TPU v7x, 32 devices: a whole 2x2x4 slice. The times are simulated.
32 devices in a mesh: parts: 2 (over y), walk: 4 (over z), slab: 2 (over x), row: 2 (over core).
Axes of the slice: x: 2, y: 2, z: 4, core: 2. Of those that a mesh axis runs over, the one named last changes fastest.
Arguments:
- walkers: bfloat16 [64, 1024, 256], P(('parts', 'walk'), ('slab', 'row')), parts along dimension 0
- trial_orbitals: bfloat16 [2048, 256], P(('parts', 'slab', 'row')), parts along dimension 0
- cholesky: bfloat16 [16, 256, 1024], P(('parts', 'slab', 'row')), parts along dimension 0, may hold values from -0.359375 to 0.359375
- branches: int32 [64], P('parts'), parts along dimension 0, may hold values from 0 to 31, as said below
- counts: int32 [8], P(('parts', 'walk')), parts along dimension 0, may hold values from 4 to 8, as said below
- field: float32 [64, 1024], P(('parts', 'walk'), ('slab', 'row')), parts along dimension 0, may hold values from 0.7 to 1.3
Outputs:
- force_bias: float32 [64, 8], P(('parts', 'walk'), ('slab', 'row')), parts along dimension 0
- exchange_energy: float32 [64, 8], P(('parts', 'walk'), ('slab', 'row')), parts along dimension 0
There are 2 independent parts, one for each index of `parts`. A program takes and returns all parts, laid end to end along the dimension named above; each array names one. Nothing has to cross between parts.
Inputs may be any that keep to these rules, and one draw needn't show every extreme that they name: `branches`: the new walkers of one walk index copy at most 2 walkers from any one walk index, and some walk index gives exactly 2 to some walk index. `counts`: at least one walk index has all 8 alive; the alive ones are the first of its walkers.
All inputs are finite; a program needn't handle non-finite values. Where the computation divides by a largest or mean magnitude, that divisor is 1e-20 or more.
Results may differ from a plain program's by a relative error of at most 0.0068.
Values may be sent and summed in bfloat16 or wider, within the bound.
A program may use at most 64 MiB of HBM per device.

v0:
```python
import functools

import jax
import jax.numpy as jnp
from jax import lax
from jax.experimental import pallas as pl
from jax.experimental.pallas import tpu as pltpu
from jax.sharding import PartitionSpec as P

ITERS = 10
EARLY = 4
MESH = pl.DeviceIdType.MESH


def split(x):
    high = x.astype(jnp.bfloat16)
    low = (x - high.astype(jnp.float32)).astype(jnp.bfloat16)
    return high, low


def dot(a, b):
    return jnp.dot(a, b, preferred_element_type=jnp.float32)


def dot3(a, b):
    ah, al = split(a)
    bh, bl = split(b)
    return dot(ah, bh) + (dot(ah, bl) + dot(al, bh))


def partner(position, step, size):
    if size & (size - 1):
        return (position + step) % size
    result, bit = 0, 1
    while bit < size:
        digit = (position // bit) % 2
        result += bit * (1 - digit if step & bit else digit)
        bit *= 2
    return result


def kernel(
    sizes, branch_in, walker_ref, trial_ref, chol_ref, field_ref, bias_ref, exch_ref,
    branch_ref, trial_t, source, outgoing, field_in, field_out, traces, squares, bias_rows, exch_rows, raw, trial, field, chol, prop, half, inter, stack, inverse,
    z_send, z_recv, x_send, x_recv, c_send, c_recv, i_send, i_recv,
    tx_send, tx_recv, tc_send, tc_recv, fx_send, fx_recv, fc_send, fc_recv, own_sem,
):
    walks, slabs, cores, slots, local = sizes
    walk, slab, core = lax.axis_index("walk"), lax.axis_index("slab"), lax.axis_index("row")
    rows, electrons = trial_ref.shape
    vectors = chol_ref.shape[0] // electrons
    mine = slab * cores + core

    def slab_peer(step):
        return lax.rem(slab + step, slabs)

    def core_peer(step):
        return lax.rem(core + step, cores)

    def slab_source(step):
        return lax.rem(slab + slabs - step, slabs)

    def core_source(step):
        return lax.rem(core + cores - step, cores)

    loads = [(branch_in, branch_ref), (walker_ref, source), (field_ref, field_in), (trial_ref, trial.at[mine]), (chol_ref, chol)]
    own = [pltpu.make_async_copy(src, dst, own_sem.at[k]) for k, (src, dst) in enumerate(loads)]
    for copy in own:
        copy.start()
    barrier = pltpu.get_barrier_semaphore()
    greeted = 0
    if local < slots:
        for step in range(1, walks):
            pl.semaphore_signal(barrier, inc=1, device_id={"walk": partner(walk, step, walks)}, device_id_type=MESH)
            greeted += 1
    for step in range(1, slabs):
        pl.semaphore_signal(barrier, inc=1, device_id={"slab": slab_peer(step)}, device_id_type=MESH)
        greeted += 1
    for step in range(1, cores):
        pl.semaphore_signal(barrier, inc=1, device_id={"row": core_peer(step)}, device_id_type=MESH)
        greeted += 1

    def sender(w, k):
        return lax.div(branch_ref[w * slots + k], slots)

    def kth(w, origin, values):
        picks, count = [jnp.int32(0)] * local, jnp.int32(0)
        for k in range(slots):
            hit = sender(w, k) == origin
            picks = [jnp.where(hit & (count == place), values(k), pick) for place, pick in enumerate(picks)]
            count = count + jnp.where(hit, 1, 0)
        return picks

    for copy in own[:3]:
        copy.wait()
    slot_of = list(range(slots))
    if local < slots:
        origins = []
        for step in range(walks):
            target = partner(walk, step, walks)
            picks = kth(target, walk, lambda k: lax.rem(branch_ref[target * slots + k], slots))
            for place, pick in enumerate(picks):
                if step == 0:
                    raw[place, mine] = source[pick]
                else:
                    outgoing[step * local + place] = source[pick]
            origin = target if walks & (walks - 1) == 0 else (walk + walks - step) % walks
            origins.append(origin)
            for place, pick in enumerate(kth(walk, origin, lambda k: k)):
                i = step * local + place
                field_out[i : i + 1, :] = field_in[pl.ds(pick, 1), :]
        for j in range(slots):
            origin, rank, step_of = sender(walk, j), jnp.int32(0), jnp.int32(0)
            for k in range(j):
                rank = rank + jnp.where(sender(walk, k) == origin, 1, 0)
            for step in range(walks):
                step_of = jnp.where(origins[step] == origin, step, step_of)
            slot_of[j] = jnp.minimum(step_of * local + rank, slots - 1)
    else:
        for i in range(slots):
            raw[i, mine] = source[i]
        field_out[...] = field_in[...]
    field[mine] = field_out[...]
    for copy in own[3:]:
        copy.wait()
    pl.semaphore_wait(barrier, greeted)

    def remote(src, dst, send, recv, target):
        return pltpu.make_async_remote_copy(
            src_ref=src, dst_ref=dst, send_sem=send, recv_sem=recv, device_id=target, device_id_type=MESH
        )

    def z_copy(i, step):
        return remote(outgoing.at[i], raw.at[i, mine], z_send.at[i], z_recv.at[i], {"walk": partner(walk, step, walks)})

    def x_copy(i, step):
        return remote(raw.at[i, mine], raw.at[i, mine], x_send.at[step, i], x_recv.at[step, i], {"slab": slab_peer(step)})

    def c_copy(i, hop, step):
        q = slab_source(hop) * cores + core
        return remote(raw.at[i, q], raw.at[i, q], c_send.at[hop, step, i], c_recv.at[hop, step, i], {"row": core_peer(step)})

    def small(src, buf, xs, xr, cs, cr):
        def x(step):
            return remote(src, buf.at[mine], xs.at[step], xr.at[step], {"slab": slab_peer(step)})

        def c(hop, step):
            q = slab_source(hop) * cores + core
            block = src if hop == 0 else buf.at[q]
            return remote(block, buf.at[q], cs.at[hop, step], cr.at[hop, step], {"row": core_peer(step)})

        return x, c

    for i in range(local, slots):
        z_copy(i, i // local).start()
    pairs = [
        small(trial_ref, trial, tx_send, tx_recv, tc_send, tc_recv),
        small(field_out, field, fx_send, fx_recv, fc_send, fc_recv),
    ]
    for x, c in pairs:
        for step in range(1, slabs):
            x(step).start()
        for step in range(1, cores):
            c(0, step).start()
    def spread(i):
        for step in range(1, slabs):
            x_copy(i, step).start()
        for step in range(1, cores):
            c_copy(i, 0, step).start()

    def relay(i):
        for hop in range(1, slabs):
            x_copy(i, hop).wait_recv()
            for step in range(1, cores):
                c_copy(i, hop, step).start()

    def compute(i):
        for hop in range(slabs):
            for step in range(1, cores):
                c_copy(i, hop, step).wait_recv()
        for q in range(slabs * cores):
            column = jnp.transpose(field[q])
            lane = lax.broadcasted_iota(jnp.int32, column.shape, 1)
            scale = jnp.sum(jnp.where(lane == i, column, 0.0), axis=1, keepdims=True)
            prop[q * rows : (q + 1) * rows, :] = (raw[i, q].astype(jnp.float32) * scale).astype(jnp.bfloat16)
        @pl.when(lax.rem(i, cores) == core)
        def _():
            total = dot(trial_t[0], prop[0:rows, :])
            for q in range(1, slabs * cores):
                total += dot(trial_t[q], prop[q * rows : (q + 1) * rows, :])
            inter[i // cores] = total

        half[i] = dot(chol[...], prop[...]).astype(jnp.bfloat16)

    for i in range(local):
        spread(i)
    for x, c in pairs:
        for hop in range(1, slabs):
            x(hop).wait_recv()
            for step in range(1, cores):
                c(hop, step).start()
    for x, c in pairs:
        for hop in range(slabs):
            for step in range(1, cores):
                c(hop, step).wait_recv()

    for q in range(slabs * cores):
        trial_t[q] = jnp.transpose(trial[q].astype(jnp.float32)).astype(jnp.bfloat16)
    share = slots // cores
    line = lax.broadcasted_iota(jnp.int32, (electrons, electrons), 0)
    diagonal = line == lax.broadcasted_iota(jnp.int32, (electrons, electrons), 1)

    def i_copy(i, step):
        place = inverse.at[i]
        return remote(place, place, i_send.at[i // cores, step], i_recv.at[i // cores, step], {"row": core_peer(step)})

    def first_guess(n):
        matrix = inter[n]
        sizes_of = jnp.abs(matrix)
        column_max = jnp.max(jnp.sum(sizes_of, axis=0, keepdims=True), axis=1, keepdims=True)
        row_max = jnp.max(jnp.sum(sizes_of, axis=1, keepdims=True), axis=0, keepdims=True)
        start = jnp.transpose(matrix) / (column_max * row_max)
        stack[0:electrons, :] = start
        stack[electrons:, :] = dot3(matrix, start)

    def finish(i):
        @pl.when(lax.rem(i, cores) != core)
        def _():
            i_copy(i, lax.rem(core + cores - lax.rem(i, cores), cores)).wait_recv()

        contracted = dot(half[i], inverse[i])
        for g in range(vectors):
            block = contracted[g * electrons : (g + 1) * electrons, :]
            traces[i, g : g + 1, :] = jnp.sum(jnp.where(diagonal, block, 0.0), axis=0, keepdims=True)
            squares[i, g : g + 1, :] = jnp.sum(block * jnp.transpose(block), axis=0, keepdims=True)

    ready = cores + 1

    @pl.loop(0, slots + ready + cores + 1)
    def _(i):
        @pl.when((i >= local) & (i < slots))
        def _():
            z_copy(i, 0).wait_recv()
            spread(i)

        @pl.when((i > 1) & (i < slots + 2))
        def _():
            compute(i - 2)

        @pl.when((i > 0) & (i <= slots))
        def _():
            relay(i - 1)

        for part in range(cores):

            @pl.when((i >= ready) & (i < slots + ready) & (lax.rem(i + cores - 1, cores) == part))
            def _():
                n = (i - ready) // cores
                if part == 0:
                    first_guess(n)

                first, middle, last = ITERS * part // cores, EARLY, ITERS * (part + 1) // cores

                @pl.loop(first, max(first, min(middle, last)))
                def _(iteration):
                    both = stack[...]
                    low = both.astype(jnp.bfloat16)
                    stack[...] = 2.0 * both - dot(low, low[electrons:, :])

                @pl.loop(min(last, max(middle, first)), last)
                def _(iteration):
                    both = stack[...]
                    stack[...] = 2.0 * both - dot3(both, both[electrons:, :])

                if part == cores - 1:
                    inverse[n * cores + core] = stack[0:electrons, :].astype(jnp.bfloat16)
                    for step in range(1, cores):
                        i_copy(n * cores + core, step).start()

        @pl.when(i > ready + cores)
        def _():
            finish(i - ready - cores - 1)


    column = lax.broadcasted_iota(jnp.int32, bias_ref.shape, 1)
    for terms, rows_of, result in ((traces, bias_rows, bias_ref), (squares, exch_rows, exch_ref)):
        for j in range(slots):
            block = terms[slot_of[j]]
            for g in range(vectors):
                rows_of[g, j : j + 1, :] = block[g : g + 1, :]
        total = jnp.zeros(result.shape, jnp.float32)
        for g in range(vectors):
            total = jnp.where(column == g, jnp.sum(rows_of[g], axis=1, keepdims=True), total)
        result[...] = total

    for i in range(local, slots):
        z_copy(i, i // local).wait_send()

    @pl.loop(0, slots)
    def _(i):
        for step in range(1, slabs):
            x_copy(i, step).wait_send()
        for hop in range(slabs):
            for step in range(1, cores):
                c_copy(i, hop, step).wait_send()

    for x, c in pairs:
        for step in range(1, slabs):
            x(step).wait_send()
        for hop in range(slabs):
            for step in range(1, cores):
                c(hop, step).wait_send()
    for n in range(share):
        for step in range(1, cores):
            i_copy(n * cores + core, step).wait_send()


def on_device(walkers, trial_orbitals, cholesky, branches, counts, field):
    walks, slabs, cores = lax.axis_size("walk"), lax.axis_size("slab"), lax.axis_size("row")
    walk = lax.axis_index("walk")
    per_device, rows, electrons = walkers.shape
    vectors = cholesky.shape[0]
    capacity = (per_device + walks - 1) // walks
    local = capacity if walks * capacity == per_device else per_device
    if local == per_device:
        sender = branches.reshape(walks, per_device) // per_device
        local_index = branches.reshape(walks, per_device) % per_device
        places = jnp.arange(per_device, dtype=jnp.int32)
        same_sender = sender[:, :, None] == sender[:, None, :]
        rank = jnp.sum(same_sender & (places[None, :] < places[:, None])[None], axis=2)
        ranks = jnp.arange(capacity, dtype=jnp.int32)[None, :, None]
        wanted = (sender[:, None, :] == walk) & (rank[:, None, :] == ranks)
        chosen = jnp.sum(jnp.where(wanted, local_index[:, None, :], 0), axis=2)
        outgoing = jnp.take(walkers, chosen.reshape(-1), axis=0, mode="clip")
        outgoing = outgoing.reshape(walks, capacity, rows, electrons)
        arrived = lax.all_to_all(outgoing, "walk", split_axis=0, concat_axis=0, tiled=True)
        arrived = arrived.reshape(walks * capacity, rows, electrons)
        my_sender = lax.dynamic_index_in_dim(sender, walk, 0, keepdims=False)
        my_rank = lax.dynamic_index_in_dim(rank, walk, 0, keepdims=False)
        walkers = jnp.take(arrived, my_sender * capacity + my_rank, axis=0, mode="clip")
    shards = slabs * cores
    share = per_device // cores
    dma = pltpu.SemaphoreType.DMA
    vmem = pl.BlockSpec(memory_space=pltpu.VMEM)
    bias, exchange = pl.pallas_call(
        functools.partial(kernel, (walks, slabs, cores, per_device, local)),
        out_shape=[jax.ShapeDtypeStruct((per_device, vectors), jnp.float32)] * 2,
        in_specs=[pl.BlockSpec(memory_space=pl.ANY)] * 5,
        out_specs=[vmem] * 2,
        scratch_shapes=[
            pltpu.SMEM(branches.shape, jnp.int32),
            pltpu.VMEM((shards, electrons, rows), jnp.bfloat16),
            pltpu.VMEM((per_device, rows, electrons), jnp.bfloat16),
            pltpu.VMEM((per_device, rows, electrons), jnp.bfloat16),
            pltpu.VMEM((per_device, rows), jnp.float32),
            pltpu.VMEM((per_device, rows), jnp.float32),
            pltpu.VMEM((per_device, vectors, electrons), jnp.float32),
            pltpu.VMEM((per_device, vectors, electrons), jnp.float32),
            pltpu.VMEM((vectors, per_device, electrons), jnp.float32),
            pltpu.VMEM((vectors, per_device, electrons), jnp.float32),
            pltpu.VMEM((per_device, shards, rows, electrons), jnp.bfloat16),
            pltpu.VMEM((shards, rows, electrons), jnp.bfloat16),
            pltpu.VMEM((shards, per_device, rows), jnp.float32),
            pltpu.VMEM((vectors * electrons, shards * rows), jnp.bfloat16),
            pltpu.VMEM((shards * rows, electrons), jnp.bfloat16),
            pltpu.VMEM((per_device, vectors * electrons, electrons), jnp.bfloat16),
            pltpu.VMEM((share, electrons, electrons), jnp.float32),
            pltpu.VMEM((2 * electrons, electrons), jnp.float32),
            pltpu.VMEM((per_device, electrons, electrons), jnp.bfloat16),
            dma((per_device,)), dma((per_device,)),
            dma((slabs, per_device)), dma((slabs, per_device)),
            dma((slabs, cores, per_device)), dma((slabs, cores, per_device)),
            dma((share, cores)), dma((share, cores)),
            dma((slabs,)), dma((slabs,)), dma((slabs, cores)), dma((slabs, cores)),
            dma((slabs,)), dma((slabs,)), dma((slabs, cores)), dma((slabs, cores)),
            dma((5,)),
        ],
        compiler_params=pltpu.CompilerParams(
            collective_id=0, has_side_effects=True, vmem_limit_bytes=63 * 1024 * 1024
        ),
    )(branches, walkers, trial_orbitals, cholesky.reshape(vectors * electrons, shards * rows), field)
    living = (jnp.arange(per_device, dtype=jnp.int32) < counts[0]).astype(jnp.float32)[:, None]
    return bias * living, -0.5 * exchange * living


def solution(mesh):
    return jax.shard_map(
        on_device,
        mesh=mesh,
        in_specs=(
            P(("parts", "walk"), ("slab", "row"), None),
            P(("parts", "slab", "row"), None),
            P(("parts", "slab", "row"), None, None),
            P("parts"),
            P(("parts", "walk")),
            P(("parts", "walk"), ("slab", "row")),
        ),
        out_specs=(P(("parts", "walk"), ("slab", "row")), P(("parts", "walk"), ("slab", "row"))),
        check_vma=False,
    )
```

profile of v0, /device:TPU:0, one launch (start us, length us, event | category | flops | bytes accessed | tf_op | source)
XLA Modules:
  0.0 49.2 jit_solution(2029062016556997710)
XLA Ops:
  1.3 45.8 %shard_map.77 = (f32[8,2]{1,0:T(8,128)}, f32[8,2]{1,0:T(8,128)}) custom-call(s32[32]{0:T(128)} %branch_in.1, bf16[8,256,256]{2,1,0:T(8,128)(2,1)} %walker_ref.1, bf16[256,256]{1,0:T(8,128)(2,1)} %trial_ref.1, bf16[512,1024]{1,0:T(8,128)(2,1)} %bitcast.4, f32[8,256]{1,0:T(8,128)} %field_ref.1), custom_call_target="tpu_custom_call" | custom-call | tf_op jit(solution)/shard_map/pallas_call | solution.py:345
  47.1 0.8 %broadcast_multiply_fusion = (f32[8,2]{1,0:T(8,128)S(1)}, f32[8,2]{1,0:T(8,128)S(1)}) fusion(f32[8,2]{1,0:T(8,128)} %get-tuple-element.5, f32[8]{0:T(128)S(1)} %compare_select_fusion, f32[8,2]{1,0:T(8,128)} %get-tuple-element.4, f32[8]{0:T(128)S(1)} %compare_convert_fusion), kind=kLoop, calls=%fused_computation | loop fusion | flops 32 | bytes 320 | tf_op jit(solution)/shard_map/mul | solution.py:383
  47.9 0.6 %copy.9 = f32[8,2]{0,1:T(2,128)} copy(f32[8,2]{1,0:T(8,128)S(1)} %get-tuple-element.8) | data formatting | bytes 128
  48.5 0.6 %copy.8 = f32[8,2]{0,1:T(2,128)} copy(f32[8,2]{1,0:T(8,128)S(1)} %get-tuple-element.9) | data formatting | bytes 128
  (2 shorter events, 0.0 us)
where the time goes:
time: 49.4 us; the launch traced here: 49.2 us
  Pallas kernels  45.8 us (93%)
  between operations  1.3 us (3%)
  local copies, waits for them, and re-layouts  1.27 us (3%)
  other arithmetic  0.76 us (2%)
    pallas_call x1, Pallas kernels, on_device(): pl.pallas_call(functools.partial(kernel, (walks, slabs, cores, per_device...  45.8 us
    unnamed x2, local copies, waits for them, and re-layouts  1.27 us

commit v1 on v0

--- a/solution.py
+++ b/solution.py
@@ -9,6 +9,8 @@
 
 ITERS = 10
 EARLY = 4
+PASSES = 6
+PIECES = 4
 MESH = pl.DeviceIdType.MESH
 
 
@@ -315,7 +317,367 @@
             i_copy(n * cores + core, step).wait_send()
 
 
-def on_device(walkers, trial_orbitals, cholesky, branches, counts, field):
+def xor(a, b, size):
+    result, bit = 0, 1
+    while bit < size:
+        left, right = lax.rem(lax.div(a, bit), 2), lax.rem(lax.div(b, bit), 2)
+        result += bit * lax.rem(left + right, 2)
+        bit *= 2
+    return result
+
+
+def origin_kernel(
+    sizes, branch_in, walker_ref, trial_ref, chol_ref, field_ref, bias_ref, exch_ref,
+    branch_ref, source, fields, chosen, outgoing, prop, trial, trial_t, chol, stack, green, lanes, sums, arrived,
+    own_sem, f_send, f_recv, t_send, t_recv, tx_send, tp_sem, cx_send, c_send, c_recv, cp_sem, w_send, w_recv, o_send, o_recv,
+):
+    walks, slabs, cores, slots, local, items = sizes
+    walk, slab, core = lax.axis_index("walk"), lax.axis_index("slab"), lax.axis_index("row")
+    rows, electrons = trial_ref.shape
+    shards = slabs * cores
+    vectors = chol_ref.shape[0] // electrons
+    mine = slab * cores + core
+    other_slab, other_core = 1 - slab, 1 - core
+    across, beside, diagonal_q = other_slab * cores + core, slab * cores + other_core, other_slab * cores + other_core
+    below, above = walk > 0, walk < walks - 1
+    steps = ((1, 1), (1, 0), (0, 1))
+
+    loads = [(branch_in, branch_ref), (walker_ref, source), (field_ref, fields.at[walk]), (trial_ref, trial.at[mine]), (chol_ref, chol.at[mine])]
+    own = [pltpu.make_async_copy(src, dst, own_sem.at[k]) for k, (src, dst) in enumerate(loads)]
+    for copy in own:
+        copy.start()
+    barrier = pltpu.get_barrier_semaphore()
+
+    def greet(target):
+        pl.semaphore_signal(barrier, inc=1, device_id=target, device_id_type=MESH)
+
+    def place_of(dx, dc):
+        return {"slab": lax.rem(slab + dx, slabs), "row": lax.rem(core + dc, cores)}
+
+    for dx, dc in steps:
+        greet(place_of(dx, dc))
+
+    @pl.when(below)
+    def _():
+        greet({"walk": walk - 1})
+
+    @pl.when(above)
+    def _():
+        greet({"walk": walk + 1})
+
+    pl.semaphore_wait(barrier, len(steps) + jnp.where(below, 1, 0) + jnp.where(above, 1, 0))
+
+    def remote(src, dst, send, recv, target):
+        return pltpu.make_async_remote_copy(
+            src_ref=src, dst_ref=dst, send_sem=send, recv_sem=recv, device_id=target, device_id_type=MESH
+        )
+
+    def field_copy(o, way):
+        block = fields.at[o]
+        src = field_ref if way[1] else block
+        return remote(src, block, f_send.at[way[0], o], f_recv.at[o], {"walk": walk + 1 - 2 * way[0]})
+
+    def trial_view(q, o):
+        size = rows // walks
+        return trial.at[q, pl.ds(pl.multiple_of(o * size, size), size)]
+
+    def chol_rows(o, p):
+        size = chol_ref.shape[0] // (walks * PIECES)
+        return pl.ds(pl.multiple_of((o * PIECES + p) * size, size), size)
+
+    def trial_copy(o, way):
+        view = trial_view(across, o)
+        if way == 2:
+            return remote(view, view, t_send.at[2, o], t_recv.at[1, o], {"row": other_core})
+        return remote(view, view, t_send.at[way, o], t_recv.at[0, o], {"walk": walk + 1 - 2 * way})
+
+    def trial_beside(o):
+        view = trial_view(diagonal_q, o)
+        return remote(view, view, t_send.at[2, o], t_recv.at[1, o], {"row": other_core})
+
+    def chol_copy(o, p, way):
+        view = chol.at[across, chol_rows(o, p)]
+        if way == 2:
+            return remote(view, view, c_send.at[2, o, p], c_recv.at[1, o, p], {"row": other_core})
+        return remote(view, view, c_send.at[way, o, p], c_recv.at[0, o, p], {"walk": walk + 1 - 2 * way})
+
+    def chol_beside(o, p):
+        view = chol.at[diagonal_q, chol_rows(o, p)]
+        return remote(view, view, c_send.at[2, o, p], c_recv.at[1, o, p], {"row": other_core})
+
+    def trial_across():
+        size = rows // walks
+        src = trial_ref.at[pl.ds(pl.multiple_of(walk * size, size), size)]
+        return remote(src, trial_view(mine, walk), tx_send.at[0], t_recv.at[0, walk], {"slab": other_slab})
+
+    def chol_across(p):
+        return remote(chol_ref.at[chol_rows(walk, p)], chol.at[mine, chol_rows(walk, p)], cx_send.at[p], c_recv.at[0, walk, p], {"slab": other_slab})
+
+    trial_whole = remote(trial_ref, trial.at[mine], tp_sem.at[0], tp_sem.at[1], {"row": other_core})
+    chol_whole = remote(chol_ref, chol.at[mine], cp_sem.at[0], cp_sem.at[1], {"row": other_core})
+
+    def both_ways(action):
+        @pl.when(above)
+        def _():
+            action(0)
+
+        @pl.when(below)
+        def _():
+            action(1)
+
+    def hop(k, arrive, forward):
+        @pl.when(walk >= k)
+        def _():
+            arrive(walk - k)
+            if k < walks - 1:
+                pl.when(above)(lambda: forward(walk - k, 0))
+
+        @pl.when(walk + k < walks)
+        def _():
+            arrive(walk + k)
+            if k < walks - 1:
+                pl.when(below)(lambda: forward(walk + k, 1))
+
+    def field_hop(k):
+        hop(k, lambda o: field_copy(o, (0, False)).wait_recv(), lambda o, way: field_copy(o, (way, False)).start())
+
+    def trial_arrive(o):
+        trial_copy(o, 0).wait_recv()
+        trial_copy(o, 2).start()
+
+    def trial_hop(k):
+        hop(k, trial_arrive, lambda o, way: trial_copy(o, way).start())
+
+    def chol_hop(k):
+        @pl.loop(0, PIECES)
+        def _(p):
+            def arrive(o):
+                chol_copy(o, p, 0).wait_recv()
+                chol_copy(o, p, 2).start()
+
+            hop(k, arrive, lambda o, way: chol_copy(o, p, way).start())
+
+    def chol_start(p):
+        chol_copy(walk, p, 0).wait_recv()
+        both_ways(lambda way: chol_copy(walk, p, way).start())
+        chol_copy(walk, p, 2).start()
+
+    both_ways(lambda way: field_copy(walk, (way, True)).start())
+    trial_across().start()
+    for p in range(PIECES):
+        chol_across(p).start()
+    trial_whole.start()
+    chol_whole.start()
+
+    field_hop(1)
+    trial_arrive(walk)
+    both_ways(lambda way: trial_copy(walk, way).start())
+    if walks > 2:
+        field_hop(2)
+    chol_start(0)
+    for k in range(3, walks):
+        field_hop(k)
+
+    def sender(w, k):
+        return lax.div(branch_ref[w * slots + k], slots)
+
+    def item_target(number):
+        step = walks - 1 - lax.div(number, local)
+        return xor(walk, step, walks), lax.rem(number, local)
+
+    def locate(number):
+        target, place = item_target(number)
+        pick, spot, count = jnp.int32(0), jnp.int32(0), jnp.int32(0)
+        for k in range(slots):
+            hit = sender(target, k) == walk
+            here = hit & (count == place)
+            pick = jnp.where(here, lax.rem(branch_ref[target * slots + k], slots), pick)
+            spot = jnp.where(here, k, spot)
+            count = count + jnp.where(hit, 1, 0)
+        return target, pick, spot
+
+    def w_copy(r, dx, dc):
+        d = dx * cores + dc
+        part = pl.ds(pl.multiple_of(mine * rows, rows), rows)
+        return remote(outgoing.at[r, d], prop.at[r, part], w_send.at[r, d], w_recv.at[r, d], place_of(dx, dc))
+
+    for copy in own[:3]:
+        copy.wait()
+    offsets = steps + ((0, 0),)
+    picks = []
+    for r in range(items):
+        for dx, dc in offsets:
+            q = lax.rem(slab + dx, slabs) * cores + lax.rem(core + dc, cores)
+            target, pick, spot = locate(r * shards + q)
+            i = len(picks)
+            picks.append(pick)
+            chosen[i : i + 1, :] = fields[target, pl.ds(spot, 1), :]
+    scales = jnp.transpose(chosen[...])
+    for r in range(items):
+        for n, (dx, dc) in enumerate(offsets):
+            i = r * shards + n
+            block = (source[picks[i]].astype(jnp.float32) * scales[:, i : i + 1]).astype(jnp.bfloat16)
+            if dx or dc:
+                outgoing[r, dx * cores + dc] = block
+                w_copy(r, dx, dc).start()
+            else:
+                prop[r, pl.ds(pl.multiple_of(mine * rows, rows), rows)] = block
+        if r + 1 < PIECES:
+            chol_start(r + 1)
+    for p in range(items + 1, PIECES):
+        chol_start(p)
+    for k in range(1, walks):
+        trial_hop(k)
+    chol_hop(1)
+
+    @pl.loop(0, walks)
+    def _(o):
+        trial_beside(o).wait_recv()
+
+    own[3].wait()
+    trial_whole.wait_recv()
+    for q in range(shards):
+        trial_t[:, q * rows : (q + 1) * rows] = jnp.transpose(trial[q].astype(jnp.float32)).astype(jnp.bfloat16)
+    for k in range(2, walks - 1):
+        chol_hop(k)
+
+    line = lax.broadcasted_iota(jnp.int32, (electrons, electrons), 0)
+    on_diagonal = line == lax.broadcasted_iota(jnp.int32, (electrons, electrons), 1)
+
+    def invert(r):
+        for dx, dc in steps:
+            w_copy(r, dx, dc).wait_recv()
+        matrix = dot(trial_t[...], prop[r])
+        sizes_of = jnp.abs(matrix)
+        column_max = jnp.max(jnp.sum(sizes_of, axis=0, keepdims=True), axis=1, keepdims=True)
+        row_max = jnp.max(jnp.sum(sizes_of, axis=1, keepdims=True), axis=0, keepdims=True)
+        start = jnp.transpose(matrix) / (column_max * row_max)
+        stack[0:electrons, :] = start
+        stack[electrons:, :] = dot3(matrix, start)
+
+        @pl.loop(0, PASSES)
+        def _(iteration):
+            both = stack[...]
+            low = both.astype(jnp.bfloat16)
+            stack[...] = 2.0 * both - dot(low, low[electrons:, :])
+
+        @pl.loop(PASSES, ITERS)
+        def _(iteration):
+            both = stack[...]
+            stack[...] = 2.0 * both - dot3(both, both[electrons:, :])
+
+        green[r] = dot(prop[r], stack[0:electrons, :].astype(jnp.bfloat16)).astype(jnp.bfloat16)
+
+    def contract(r, q):
+        for g in range(vectors):
+            block = dot(chol[q, g * electrons : (g + 1) * electrons, :], green[r])
+            number = q * vectors + g
+            lanes[r, 0, pl.ds(number, 1), :] = jnp.sum(jnp.where(on_diagonal, block, 0.0), axis=0, keepdims=True)
+            lanes[r, 1, pl.ds(number, 1), :] = jnp.sum(block * jnp.transpose(block), axis=0, keepdims=True)
+
+    def o_copy(r, dx, dc):
+        number = r * shards + mine
+        target, _ = item_target(number)
+        device = {"walk": target, **place_of(dx, dc)}
+        return target, remote(sums.at[r], arrived.at[number], o_send.at[r, dx * cores + dc], o_recv.at[number], device)
+
+    def publish(r):
+        for kind in range(2):
+            total = jnp.sum(lanes[r, kind], axis=1, keepdims=True)
+            sums[r, kind] = jnp.broadcast_to(total, sums.shape[2:])
+        for dx, dc in steps:
+            o_copy(r, dx, dc)[1].start()
+        target, copy = o_copy(r, 0, 0)
+        pl.when(target != walk)(copy.start)
+
+        @pl.when(target == walk)
+        def _():
+            arrived[r * shards + mine] = sums[r]
+
+    invert(0)
+    own[4].wait()
+    contract(0, mine)
+    chol_whole.wait_recv()
+    contract(0, beside)
+    if walks > 1:
+        chol_hop(walks - 1)
+    for r in range(1, items):
+        invert(r)
+
+    @pl.loop(0, walks)
+    def _(o):
+        @pl.loop(0, PIECES)
+        def _(p):
+            chol_beside(o, p).wait_recv()
+
+    contract(0, across)
+    contract(0, diagonal_q)
+    publish(0)
+    for r in range(1, items):
+        for q in (mine, beside, across, diagonal_q):
+            contract(r, q)
+        publish(r)
+
+    def number_of(j):
+        origin, rank = sender(walk, j), jnp.int32(0)
+        for k in range(j):
+            rank = rank + jnp.where(sender(walk, k) == origin, 1, 0)
+        step = jnp.int32(0)
+        for s in range(walks):
+            step = jnp.where(xor(walk, s, walks) == origin, s, step)
+        return jnp.clip((walks - 1 - step) * local + rank, 0, slots - 1)
+
+    numbers = [number_of(j) for j in range(slots)]
+
+    for number in range(slots):
+        target, _ = item_target(number)
+        from_me = (target == walk) & (mine == number % shards)
+
+        @pl.when(jnp.logical_not(from_me))
+        def _():
+            remote(sums.at[0], arrived.at[number], o_send.at[0, 0], o_recv.at[number], {"row": other_core}).wait_recv()
+
+    column = lax.broadcasted_iota(jnp.int32, (1, vectors), 1)
+    for j in range(slots):
+        for kind, result in enumerate((bias_ref, exch_ref)):
+            total = jnp.zeros((1, vectors), jnp.float32)
+            for g in range(vectors):
+                value = arrived[numbers[j], kind, pl.ds(mine * vectors + g, 1), 0:vectors]
+                total = jnp.where(column == g, value, total)
+            result[j : j + 1, :] = total
+
+    trial_across().wait_send()
+    trial_whole.wait_send()
+    chol_whole.wait_send()
+    for p in range(PIECES):
+        chol_across(p).wait_send()
+
+    @pl.loop(0, walks)
+    def _(o):
+        trial_copy(o, 2).wait_send()
+
+        def sent(way):
+            field_copy(o, (way, False)).wait_send()
+            trial_copy(o, way).wait_send()
+
+        pl.when(above & (o <= walk))(lambda: sent(0))
+        pl.when(below & (o >= walk))(lambda: sent(1))
+
+        @pl.loop(0, PIECES)
+        def _(p):
+            chol_copy(o, p, 2).wait_send()
+            pl.when(above & (o <= walk))(lambda: chol_copy(o, p, 0).wait_send())
+            pl.when(below & (o >= walk))(lambda: chol_copy(o, p, 1).wait_send())
+
+    for r in range(items):
+        for dx, dc in steps:
+            w_copy(r, dx, dc).wait_send()
+            o_copy(r, dx, dc)[1].wait_send()
+        target, copy = o_copy(r, 0, 0)
+        pl.when(target != walk)(copy.wait_send)
+
+
+def gathered(walkers, trial_orbitals, cholesky, branches, field):
     walks, slabs, cores = lax.axis_size("walk"), lax.axis_size("slab"), lax.axis_size("row")
     walk = lax.axis_index("walk")
     per_device, rows, electrons = walkers.shape
@@ -379,7 +741,61 @@
             collective_id=0, has_side_effects=True, vmem_limit_bytes=63 * 1024 * 1024
         ),
     )(branches, walkers, trial_orbitals, cholesky.reshape(vectors * electrons, shards * rows), field)
-    living = (jnp.arange(per_device, dtype=jnp.int32) < counts[0]).astype(jnp.float32)[:, None]
+    return bias, exchange
+
+
+def at_origin(walkers, trial_orbitals, cholesky, branches, field):
+    walks, slabs, cores = lax.axis_size("walk"), lax.axis_size("slab"), lax.axis_size("row")
+    slots, rows, electrons = walkers.shape
+    vectors = cholesky.shape[0]
+    shards, local = slabs * cores, slots // walks
+    items, lines, columns = slots // shards, vectors * electrons, shards * rows
+    dma = pltpu.SemaphoreType.DMA
+    vmem = pl.BlockSpec(memory_space=pltpu.VMEM)
+    return pl.pallas_call(
+        functools.partial(origin_kernel, (walks, slabs, cores, slots, local, items)),
+        out_shape=[jax.ShapeDtypeStruct((slots, vectors), jnp.float32)] * 2,
+        in_specs=[pl.BlockSpec(memory_space=pl.ANY)] * 5,
+        out_specs=[vmem] * 2,
+        scratch_shapes=[
+            pltpu.SMEM(branches.shape, jnp.int32),
+            pltpu.VMEM((slots, rows, electrons), jnp.bfloat16),
+            pltpu.VMEM((walks, slots, rows), jnp.float32),
+            pltpu.VMEM((slots, rows), jnp.float32),
+            pltpu.VMEM((items, shards, rows, electrons), jnp.bfloat16),
+            pltpu.VMEM((items, columns, electrons), jnp.bfloat16),
+            pltpu.VMEM((shards, rows, electrons), jnp.bfloat16),
+            pltpu.VMEM((electrons, columns), jnp.bfloat16),
+            pltpu.VMEM((shards, lines, columns), jnp.bfloat16),
+            pltpu.VMEM((2 * electrons, electrons), jnp.float32),
+            pltpu.VMEM((items, columns, electrons), jnp.bfloat16),
+            pltpu.VMEM((items, 2, shards * vectors, electrons), jnp.float32),
+            pltpu.VMEM((items, 2, shards * vectors, 128), jnp.float32),
+            pltpu.VMEM((slots, 2, shards * vectors, 128), jnp.float32),
+            dma((5,)),
+            dma((2, walks)), dma((walks,)),
+            dma((3, walks)), dma((2, walks)), dma((2,)), dma((2,)),
+            dma((PIECES,)), dma((3, walks, PIECES)), dma((2, walks, PIECES)), dma((2,)),
+            dma((items, shards)), dma((items, shards)),
+            dma((items, shards)), dma((slots,)),
+        ],
+        compiler_params=pltpu.CompilerParams(
+            collective_id=0, has_side_effects=True, vmem_limit_bytes=60 * 1024 * 1024
+        ),
+    )(branches, walkers, trial_orbitals, cholesky.reshape(lines, columns), field)
+
+
+def on_device(walkers, trial_orbitals, cholesky, branches, counts, field):
+    walks, slabs, cores = lax.axis_size("walk"), lax.axis_size("slab"), lax.axis_size("row")
+    slots, rows, electrons = walkers.shape
+    lines = cholesky.shape[0] * electrons
+    even = walks & (walks - 1) == 0 and slots % walks == 0 and slots % (slabs * cores) == 0
+    whole = lines % (walks * PIECES * 16) == 0 and rows % (walks * 16) == 0
+    if slabs == cores == 2 and even and whole:
+        bias, exchange = at_origin(walkers, trial_orbitals, cholesky, branches, field)
+    else:
+        bias, exchange = gathered(walkers, trial_orbitals, cholesky, branches, field)
+    living = (jnp.arange(slots, dtype=jnp.int32) < counts[0]).astype(jnp.float32)[:, None]
     return bias * living, -0.5 * exchange * living
 
 

time: 49.4 us -> 46.6 us (0.943)
  Pallas kernels: 45.8 us -> 43.1 us
    pallas_call x1, Pallas kernels: 45.8 us -> 43.1 us  [at_origin(): pl.pallas_call(functools.partial(origin_kernel, (walks, slabs, cores, slo...]
where the time goes in v1:
time: 46.6 us; the launch traced here: 46.4 us
  Pallas kernels  43.1 us (92%)
  between operations  1.3 us (3%)
  local copies, waits for them, and re-layouts  1.27 us (3%)
  other arithmetic  0.76 us (2%)
    pallas_call x1, Pallas kernels, at_origin(): pl.pallas_call(functools.partial(origin_kernel, (walks, slabs, cores, slo...  43.1 us
    unnamed x2, local copies, waits for them, and re-layouts  1.27 us

profile of v1, /device:TPU:0, one launch (start us, length us, event | category | flops | bytes accessed | tf_op | source)
XLA Modules:
  0.0 46.4 jit_solution(1064601403009846855)
XLA Ops:
  1.3 43.1 %shard_map.77 = (f32[8,2]{1,0:T(8,128)}, f32[8,2]{1,0:T(8,128)}) custom-call(s32[32]{0:T(128)} %branch_in.1, bf16[8,256,256]{2,1,0:T(8,128)(2,1)} %walker_ref.1, bf16[256,256]{1,0:T(8,128)(2,1)} %trial_ref.1, bf16[512,1024]{1,0:T(8,128)(2,1)} %bitcast.4, f32[8,256]{1,0:T(8,128)} %field_ref.1), custom_call_target="tpu_custom_call" | custom-call | tf_op jit(solution)/shard_map/pallas_call | solution.py:755
  44.4 0.8 %broadcast_multiply_fusion = (f32[8,2]{1,0:T(8,128)S(1)}, f32[8,2]{1,0:T(8,128)S(1)}) fusion(f32[8,2]{1,0:T(8,128)} %get-tuple-element.5, f32[8]{0:T(128)S(1)} %compare_select_fusion, f32[8,2]{1,0:T(8,128)} %get-tuple-element.4, f32[8]{0:T(128)S(1)} %compare_convert_fusion), kind=kLoop, calls=%fused_computation | loop fusion | flops 32 | bytes 320 | tf_op jit(solution)/shard_map/mul | solution.py:799
  45.1 0.6 %copy.9 = f32[8,2]{0,1:T(2,128)} copy(f32[8,2]{1,0:T(8,128)S(1)} %get-tuple-element.8) | data formatting | bytes 128
  45.8 0.6 %copy.8 = f32[8,2]{0,1:T(2,128)} copy(f32[8,2]{1,0:T(8,128)S(1)} %get-tuple-element.9) | data formatting | bytes 128
  (2 shorter events, 0.0 us)

commit v2 on v1

--- a/solution.py
+++ b/solution.py
@@ -327,8 +327,8 @@
 
 
 def origin_kernel(
-    sizes, branch_in, walker_ref, trial_ref, chol_ref, field_ref, bias_ref, exch_ref,
-    branch_ref, source, fields, chosen, outgoing, prop, trial, trial_t, chol, stack, green, lanes, sums, arrived,
+    sizes, branch_in, count_in, walker_ref, trial_ref, chol_ref, field_ref, bias_ref, exch_ref,
+    branch_ref, count_ref, source, fields, chosen, outgoing, prop, trial, trial_t, chol, stack, green, lanes, sums, arrived,
     own_sem, f_send, f_recv, t_send, t_recv, tx_send, tp_sem, cx_send, c_send, c_recv, cp_sem, w_send, w_recv, o_send, o_recv,
 ):
     walks, slabs, cores, slots, local, items = sizes
@@ -342,7 +342,7 @@
     below, above = walk > 0, walk < walks - 1
     steps = ((1, 1), (1, 0), (0, 1))
 
-    loads = [(branch_in, branch_ref), (walker_ref, source), (field_ref, fields.at[walk]), (trial_ref, trial.at[mine]), (chol_ref, chol.at[mine])]
+    loads = [(branch_in, branch_ref), (count_in, count_ref), (walker_ref, source), (field_ref, fields.at[walk]), (trial_ref, trial.at[mine]), (chol_ref, chol.at[mine])]
     own = [pltpu.make_async_copy(src, dst, own_sem.at[k]) for k, (src, dst) in enumerate(loads)]
     for copy in own:
         copy.start()
@@ -365,6 +365,8 @@
     def _():
         greet({"walk": walk + 1})
 
+    for copy in own:
+        copy.wait()
     pl.semaphore_wait(barrier, len(steps) + jnp.where(below, 1, 0) + jnp.where(above, 1, 0))
 
     def remote(src, dst, send, recv, target):
@@ -373,9 +375,7 @@
         )
 
     def field_copy(o, way):
-        block = fields.at[o]
-        src = field_ref if way[1] else block
-        return remote(src, block, f_send.at[way[0], o], f_recv.at[o], {"walk": walk + 1 - 2 * way[0]})
+        return remote(fields.at[o], fields.at[o], f_send.at[way, o], f_recv.at[o], {"walk": walk + 1 - 2 * way})
 
     def trial_view(q, o):
         size = rows // walks
@@ -406,15 +406,13 @@
         return remote(view, view, c_send.at[2, o, p], c_recv.at[1, o, p], {"row": other_core})
 
     def trial_across():
-        size = rows // walks
-        src = trial_ref.at[pl.ds(pl.multiple_of(walk * size, size), size)]
-        return remote(src, trial_view(mine, walk), tx_send.at[0], t_recv.at[0, walk], {"slab": other_slab})
+        return remote(trial_view(mine, walk), trial_view(mine, walk), tx_send.at[0], t_recv.at[0, walk], {"slab": other_slab})
 
     def chol_across(p):
-        return remote(chol_ref.at[chol_rows(walk, p)], chol.at[mine, chol_rows(walk, p)], cx_send.at[p], c_recv.at[0, walk, p], {"slab": other_slab})
-
-    trial_whole = remote(trial_ref, trial.at[mine], tp_sem.at[0], tp_sem.at[1], {"row": other_core})
-    chol_whole = remote(chol_ref, chol.at[mine], cp_sem.at[0], cp_sem.at[1], {"row": other_core})
+        return remote(chol.at[mine, chol_rows(walk, p)], chol.at[mine, chol_rows(walk, p)], cx_send.at[p], c_recv.at[0, walk, p], {"slab": other_slab})
+
+    trial_whole = remote(trial.at[mine], trial.at[mine], tp_sem.at[0], tp_sem.at[1], {"row": other_core})
+    chol_whole = remote(chol.at[mine], chol.at[mine], cp_sem.at[0], cp_sem.at[1], {"row": other_core})
 
     def both_ways(action):
         @pl.when(above)
@@ -439,7 +437,7 @@
                 pl.when(below)(lambda: forward(walk + k, 1))
 
     def field_hop(k):
-        hop(k, lambda o: field_copy(o, (0, False)).wait_recv(), lambda o, way: field_copy(o, (way, False)).start())
+        hop(k, lambda o: field_copy(o, 0).wait_recv(), lambda o, way: field_copy(o, way).start())
 
     def trial_arrive(o):
         trial_copy(o, 0).wait_recv()
@@ -448,45 +446,30 @@
     def trial_hop(k):
         hop(k, trial_arrive, lambda o, way: trial_copy(o, way).start())
 
-    def chol_hop(k):
-        @pl.loop(0, PIECES)
-        def _(p):
-            def arrive(o):
-                chol_copy(o, p, 0).wait_recv()
-                chol_copy(o, p, 2).start()
-
-            hop(k, arrive, lambda o, way: chol_copy(o, p, way).start())
+    def chol_hop(k, p):
+        def arrive(o):
+            chol_copy(o, p, 0).wait_recv()
+            chol_copy(o, p, 2).start()
+
+        hop(k, arrive, lambda o, way: chol_copy(o, p, way).start())
 
     def chol_start(p):
         chol_copy(walk, p, 0).wait_recv()
         both_ways(lambda way: chol_copy(walk, p, way).start())
         chol_copy(walk, p, 2).start()
 
-    both_ways(lambda way: field_copy(walk, (way, True)).start())
-    trial_across().start()
-    for p in range(PIECES):
-        chol_across(p).start()
-    trial_whole.start()
-    chol_whole.start()
-
-    field_hop(1)
-    trial_arrive(walk)
-    both_ways(lambda way: trial_copy(walk, way).start())
-    if walks > 2:
-        field_hop(2)
-    chol_start(0)
-    for k in range(3, walks):
-        field_hop(k)
-
     def sender(w, k):
         return lax.div(branch_ref[w * slots + k], slots)
 
+    def step_of(number):
+        order = lax.div(number, shards) * cores + lax.rem(number, cores)
+        return walks - 1 - order, lax.div(lax.rem(number, shards), cores)
+
     def item_target(number):
-        step = walks - 1 - lax.div(number, local)
-        return xor(walk, step, walks), lax.rem(number, local)
+        return xor(walk, step_of(number)[0], walks)
 
     def locate(number):
-        target, place = item_target(number)
+        target, place = item_target(number), step_of(number)[1]
         pick, spot, count = jnp.int32(0), jnp.int32(0), jnp.int32(0)
         for k in range(slots):
             hit = sender(target, k) == walk
@@ -496,57 +479,80 @@
             count = count + jnp.where(hit, 1, 0)
         return target, pick, spot
 
-    def w_copy(r, dx, dc):
-        d = dx * cores + dc
-        part = pl.ds(pl.multiple_of(mine * rows, rows), rows)
-        return remote(outgoing.at[r, d], prop.at[r, part], w_send.at[r, d], w_recv.at[r, d], place_of(dx, dc))
-
-    for copy in own[:3]:
-        copy.wait()
-    offsets = steps + ((0, 0),)
-    picks = []
-    for r in range(items):
-        for dx, dc in offsets:
-            q = lax.rem(slab + dx, slabs) * cores + lax.rem(core + dc, cores)
-            target, pick, spot = locate(r * shards + q)
-            i = len(picks)
-            picks.append(pick)
-            chosen[i : i + 1, :] = fields[target, pl.ds(spot, 1), :]
-    scales = jnp.transpose(chosen[...])
-    for r in range(items):
-        for n, (dx, dc) in enumerate(offsets):
-            i = r * shards + n
-            block = (source[picks[i]].astype(jnp.float32) * scales[:, i : i + 1]).astype(jnp.bfloat16)
-            if dx or dc:
-                outgoing[r, dx * cores + dc] = block
-                w_copy(r, dx, dc).start()
+    slot_line = lax.broadcasted_iota(jnp.int32, (slots, rows), 0)
+    my_rows = pl.ds(pl.multiple_of(mine * rows, rows), rows)
+
+    def w_copy(r, dx, row):
+        place = {"slab": lax.rem(slab + dx, slabs), "row": row}
+        return remote(outgoing.at[r, dx * cores + row], prop.at[r, my_rows], w_send.at[r, dx * cores + row], w_recv.at[r, mine], place)
+
+    def send_group(r, row):
+        found = []
+        for dx in range(slabs):
+            target, pick, spot = locate(r * shards + lax.rem(slab + dx, slabs) * cores + row)
+            found.append(pick)
+            chosen[dx : dx + 1, :] = jnp.sum(jnp.where(slot_line == spot, fields[target], 0.0), axis=0, keepdims=True)
+        scales = jnp.transpose(chosen[...])
+        for dx in reversed(range(slabs)):
+            block = (source[found[dx]].astype(jnp.float32) * scales[:, dx : dx + 1]).astype(jnp.bfloat16)
+            outgoing[r, dx * cores + row] = block
+            if dx:
+                w_copy(r, dx, row).start()
             else:
-                prop[r, pl.ds(pl.multiple_of(mine * rows, rows), rows)] = block
-        if r + 1 < PIECES:
-            chol_start(r + 1)
-    for p in range(items + 1, PIECES):
-        chol_start(p)
-    for k in range(1, walks):
+                pl.when(core != row)(w_copy(r, dx, row).start)
+
+                @pl.when(core == row)
+                def _():
+                    prop[r, my_rows] = outgoing[r, row]
+
+    both_ways(lambda way: field_copy(walk, way).start())
+    trial_across().start()
+    for p in range(PIECES):
+        chol_across(p).start()
+    trial_whole.start()
+    chol_whole.start()
+
+    last = walks - 1
+    field_hop(1)
+    trial_arrive(walk)
+    both_ways(lambda way: trial_copy(walk, way).start())
+    chol_start(0)
+    for k in range(2, last):
+        field_hop(k)
+    send_group(0, 1)
+    trial_hop(1)
+    chol_start(1)
+    chol_start(2)
+    if last > 1:
+        field_hop(last)
+    send_group(0, 0)
+    if last > 1:
+        trial_hop(2)
+    send_group(1, 0)
+    send_group(1, 1)
+    chol_start(3)
+    for k in range(1, last - 1):
+        for p in range(PIECES):
+            chol_hop(k, p)
+    for k in range(3, walks):
         trial_hop(k)
-    chol_hop(1)
 
     @pl.loop(0, walks)
     def _(o):
         trial_beside(o).wait_recv()
 
-    own[3].wait()
     trial_whole.wait_recv()
     for q in range(shards):
         trial_t[:, q * rows : (q + 1) * rows] = jnp.transpose(trial[q].astype(jnp.float32)).astype(jnp.bfloat16)
-    for k in range(2, walks - 1):
-        chol_hop(k)
 
     line = lax.broadcasted_iota(jnp.int32, (electrons, electrons), 0)
     on_diagonal = line == lax.broadcasted_iota(jnp.int32, (electrons, electrons), 1)
 
-    def invert(r):
-        for dx, dc in steps:
-            w_copy(r, dx, dc).wait_recv()
+    def invert(r, hooks):
+        for q in (beside, across, diagonal_q):
+            part = pl.ds(pl.multiple_of(q * rows, rows), rows)
+            remote(prop.at[r, part], prop.at[r, part], w_send.at[r, 0], w_recv.at[r, q], {"row": other_core}).wait_recv()
+        hooks[0]()
         matrix = dot(trial_t[...], prop[r])
         sizes_of = jnp.abs(matrix)
         column_max = jnp.max(jnp.sum(sizes_of, axis=0, keepdims=True), axis=1, keepdims=True)
@@ -555,29 +561,36 @@
         stack[0:electrons, :] = start
         stack[electrons:, :] = dot3(matrix, start)
 
+        hooks[1]()
+
         @pl.loop(0, PASSES)
         def _(iteration):
             both = stack[...]
             low = both.astype(jnp.bfloat16)
             stack[...] = 2.0 * both - dot(low, low[electrons:, :])
 
+        hooks[2]()
+
         @pl.loop(PASSES, ITERS)
         def _(iteration):
             both = stack[...]
             stack[...] = 2.0 * both - dot3(both, both[electrons:, :])
 
+        hooks[3]()
         green[r] = dot(prop[r], stack[0:electrons, :].astype(jnp.bfloat16)).astype(jnp.bfloat16)
 
-    def contract(r, q):
+    blocks = (mine, beside, across, diagonal_q)
+
+    def contract(r, n):
         for g in range(vectors):
-            block = dot(chol[q, g * electrons : (g + 1) * electrons, :], green[r])
-            number = q * vectors + g
-            lanes[r, 0, pl.ds(number, 1), :] = jnp.sum(jnp.where(on_diagonal, block, 0.0), axis=0, keepdims=True)
-            lanes[r, 1, pl.ds(number, 1), :] = jnp.sum(block * jnp.transpose(block), axis=0, keepdims=True)
+            block = dot(chol[blocks[n], g * electrons : (g + 1) * electrons, :], green[r])
+            number = n * vectors + g
+            lanes[r, 0, number : number + 1, :] = jnp.sum(jnp.where(on_diagonal, block, 0.0), axis=0, keepdims=True)
+            lanes[r, 1, number : number + 1, :] = jnp.sum(block * jnp.transpose(block), axis=0, keepdims=True)
 
     def o_copy(r, dx, dc):
         number = r * shards + mine
-        target, _ = item_target(number)
+        target = item_target(number)
         device = {"walk": target, **place_of(dx, dc)}
         return target, remote(sums.at[r], arrived.at[number], o_send.at[r, dx * cores + dc], o_recv.at[number], device)
 
@@ -594,15 +607,16 @@
         def _():
             arrived[r * shards + mine] = sums[r]
 
-    invert(0)
-    own[4].wait()
-    contract(0, mine)
+    def hooks_of(k):
+        return [functools.partial(chol_hop, k, p) for p in range(PIECES)] if k > 0 else [lambda: None] * PIECES
+
+    invert(0, hooks_of(last - 1))
+    contract(0, 0)
     chol_whole.wait_recv()
-    contract(0, beside)
-    if walks > 1:
-        chol_hop(walks - 1)
+    contract(0, 1)
     for r in range(1, items):
-        invert(r)
+        invert(r, hooks_of(last) if r == 1 else hooks_of(0))
+    contract(0, 2)
 
     @pl.loop(0, walks)
     def _(o):
@@ -610,12 +624,11 @@
         def _(p):
             chol_beside(o, p).wait_recv()
 
-    contract(0, across)
-    contract(0, diagonal_q)
+    contract(0, 3)
     publish(0)
     for r in range(1, items):
-        for q in (mine, beside, across, diagonal_q):
-            contract(r, q)
+        for n in range(shards):
+            contract(r, n)
         publish(r)
 
     def number_of(j):
@@ -625,26 +638,29 @@
         step = jnp.int32(0)
         for s in range(walks):
             step = jnp.where(xor(walk, s, walks) == origin, s, step)
-        return jnp.clip((walks - 1 - step) * local + rank, 0, slots - 1)
+        order = walks - 1 - step
+        number = lax.div(order, cores) * shards + lax.min(rank, local - 1) * cores + lax.rem(order, cores)
+        return jnp.clip(number, 0, slots - 1)
 
     numbers = [number_of(j) for j in range(slots)]
 
     for number in range(slots):
-        target, _ = item_target(number)
+        target = item_target(number)
         from_me = (target == walk) & (mine == number % shards)
 
         @pl.when(jnp.logical_not(from_me))
         def _():
             remote(sums.at[0], arrived.at[number], o_send.at[0, 0], o_recv.at[number], {"row": other_core}).wait_recv()
 
-    column = lax.broadcasted_iota(jnp.int32, (1, vectors), 1)
-    for j in range(slots):
-        for kind, result in enumerate((bias_ref, exch_ref)):
-            total = jnp.zeros((1, vectors), jnp.float32)
-            for g in range(vectors):
-                value = arrived[numbers[j], kind, pl.ds(mine * vectors + g, 1), 0:vectors]
-                total = jnp.where(column == g, value, total)
-            result[j : j + 1, :] = total
+    column = lax.broadcasted_iota(jnp.int32, bias_ref.shape, 1)
+    for kind, result in enumerate((bias_ref, exch_ref)):
+        total = jnp.zeros(result.shape, jnp.float32)
+        for j in range(slots):
+            q = lax.rem(numbers[j], shards)
+            dx, dc = lax.rem(lax.div(q, cores) + slab, slabs), lax.rem(lax.rem(q, cores) + core, cores)
+            first = (dx * cores + dc) * vectors
+            total = jnp.where(column == j, arrived[numbers[j], kind, pl.ds(first, vectors), 0:slots], total)
+        result[...] = jnp.where(column < count_ref[0], total * (1.0, -0.5)[kind], 0.0)
 
     trial_across().wait_send()
     trial_whole.wait_send()
@@ -657,7 +673,7 @@
         trial_copy(o, 2).wait_send()
 
         def sent(way):
-            field_copy(o, (way, False)).wait_send()
+            field_copy(o, way).wait_send()
             trial_copy(o, way).wait_send()
 
         pl.when(above & (o <= walk))(lambda: sent(0))
@@ -671,10 +687,13 @@
 
     for r in range(items):
         for dx, dc in steps:
-            w_copy(r, dx, dc).wait_send()
             o_copy(r, dx, dc)[1].wait_send()
         target, copy = o_copy(r, 0, 0)
         pl.when(target != walk)(copy.wait_send)
+        for row in range(cores):
+            for dx in range(1, slabs):
+                w_copy(r, dx, row).wait_send()
+            pl.when(core != row)(w_copy(r, 0, row).wait_send)
 
 
 def gathered(walkers, trial_orbitals, cholesky, branches, field):
@@ -744,7 +763,7 @@
     return bias, exchange
 
 
-def at_origin(walkers, trial_orbitals, cholesky, branches, field):
+def at_origin(walkers, trial_orbitals, cholesky, branches, counts, field):
     walks, slabs, cores = lax.axis_size("walk"), lax.axis_size("slab"), lax.axis_size("row")
     slots, rows, electrons = walkers.shape
     vectors = cholesky.shape[0]
@@ -752,13 +771,14 @@
     items, lines, columns = slots // shards, vectors * electrons, shards * rows
     dma = pltpu.SemaphoreType.DMA
     vmem = pl.BlockSpec(memory_space=pltpu.VMEM)
-    return pl.pallas_call(
+    bias, exchange = pl.pallas_call(
         functools.partial(origin_kernel, (walks, slabs, cores, slots, local, items)),
-        out_shape=[jax.ShapeDtypeStruct((slots, vectors), jnp.float32)] * 2,
-        in_specs=[pl.BlockSpec(memory_space=pl.ANY)] * 5,
+        out_shape=[jax.ShapeDtypeStruct((vectors, slots), jnp.float32)] * 2,
+        in_specs=[pl.BlockSpec(memory_space=pl.ANY)] * 6,
         out_specs=[vmem] * 2,
         scratch_shapes=[
             pltpu.SMEM(branches.shape, jnp.int32),
+            pltpu.SMEM(counts.shape, jnp.int32),
             pltpu.VMEM((slots, rows, electrons), jnp.bfloat16),
             pltpu.VMEM((walks, slots, rows), jnp.float32),
             pltpu.VMEM((slots, rows), jnp.float32),
@@ -772,7 +792,7 @@
             pltpu.VMEM((items, 2, shards * vectors, electrons), jnp.float32),
             pltpu.VMEM((items, 2, shards * vectors, 128), jnp.float32),
             pltpu.VMEM((slots, 2, shards * vectors, 128), jnp.float32),
-            dma((5,)),
+            dma((6,)),
             dma((2, walks)), dma((walks,)),
             dma((3, walks)), dma((2, walks)), dma((2,)), dma((2,)),
             dma((PIECES,)), dma((3, walks, PIECES)), dma((2, walks, PIECES)), dma((2,)),
@@ -782,7 +802,8 @@
         compiler_params=pltpu.CompilerParams(
             collective_id=0, has_side_effects=True, vmem_limit_bytes=60 * 1024 * 1024
         ),
-    )(branches, walkers, trial_orbitals, cholesky.reshape(lines, columns), field)
+    )(branches, counts, walkers, trial_orbitals, cholesky.reshape(lines, columns), field)
+    return bias.T, exchange.T
 
 
 def on_device(walkers, trial_orbitals, cholesky, branches, counts, field):
@@ -791,10 +812,9 @@
     lines = cholesky.shape[0] * electrons
     even = walks & (walks - 1) == 0 and slots % walks == 0 and slots % (slabs * cores) == 0
     whole = lines % (walks * PIECES * 16) == 0 and rows % (walks * 16) == 0
-    if slabs == cores == 2 and even and whole:
-        bias, exchange = at_origin(walkers, trial_orbitals, cholesky, branches, field)
-    else:
-        bias, exchange = gathered(walkers, trial_orbitals, cholesky, branches, field)
+    if slabs == cores == 2 and slots == 2 * walks and PIECES == 4 and even and whole:
+        return at_origin(walkers, trial_orbitals, cholesky, branches, counts, field)
+    bias, exchange = gathered(walkers, trial_orbitals, cholesky, branches, field)
     living = (jnp.arange(slots, dtype=jnp.int32) < counts[0]).astype(jnp.float32)[:, None]
     return bias * living, -0.5 * exchange * living
 

time: 46.6 us -> 41.6 us (0.89)
  Pallas kernels: 43.1 us -> 38.2 us
  other arithmetic: 0.76 us -> 0 us
  local copies, waits for them, and re-layouts: 1.27 us -> 1.85 us
    pallas_call x1, Pallas kernels: 43.1 us -> 38.2 us  [at_origin(): pl.pallas_call(functools.partial(origin_kernel, (walks, slabs, cores, slo...]
    mul x2 -> x0, other arithmetic: 0.76 us -> none  [on_device(): return (bias * living, -0.5 * exchange * living)]
    unnamed x2 -> x6, local copies, waits for them, and re-layouts: 1.27 us -> 1.85 us
where the time goes in v2:
time: 41.6 us; the launch traced here: 41.4 us
  Pallas kernels  38.2 us (92%)
  local copies, waits for them, and re-layouts  1.85 us (4%)
  between operations  1.3 us (3%)
    pallas_call x1, Pallas kernels, at_origin(): pl.pallas_call(functools.partial(origin_kernel, (walks, slabs, cores, slo...  38.2 us
    unnamed x6, local copies, waits for them, and re-layouts  1.85 us

profile of v2, /device:TPU:0, one launch (start us, length us, event | category | flops | bytes accessed | tf_op | source)
XLA Modules:
  0.0 41.4 jit_solution(16965447056365371260)
XLA Ops:
  1.3 38.2 %shard_map.77 = (f32[2,8]{1,0:T(2,128)}, f32[2,8]{1,0:T(2,128)}) custom-call(s32[32]{0:T(128)} %branch_in.1, s32[1]{0:T(128)S(6)} %copy.10.count_in, bf16[8,256,256]{2,1,0:T(8,128)(2,1)} %walker_ref.1, bf16[256,256]{1,0:T(8,128)(2,1)} %trial_ref.1, bf16[512,1024]{1,0:T(8,128)(2,1)} %bitcast.3, f32[8,256]{1,0:T(8,128)} %field_ref.1), custom_call_target="tpu_custom_call" | custom-call | tf_op jit(solution)/shard_map/pallas_call | solution.py:774
  39.5 0.0 copy-start.1
  39.5 0.7 %copy-done.1 = f32[2,8]{1,0:T(2,128)S(1)} copy-done((f32[2,8]{1,0:T(2,128)S(1)}, f32[2,8]{1,0:T(2,128)}, u32[]{:S(2)}) %copy-start.1) | copy-done | bytes 88
  40.2 0.0 copy-start
  40.2 0.6 %copy.11 = f32[8,2]{0,1:T(2,128)} copy(f32[8,2]{0,1:T(2,128)S(1)} %bitcast.5) | data formatting | bytes 128
  40.8 0.1 copy-done
  40.8 0.6 %copy.12 = f32[8,2]{0,1:T(2,128)} copy(f32[8,2]{0,1:T(2,128)S(1)} %bitcast.4) | data formatting | bytes 128
Async XLA Ops:
  39.5 0.7 %copy-start.1 = (f32[2,8]{1,0:T(2,128)S(1)}, f32[2,8]{1,0:T(2,128)}, u32[]{:S(2)}) copy-start(f32[2,8]{1,0:T(2,128)} %get-tuple-element.4) | copy-start | bytes 196
  40.2 0.6 %copy-start = (f32[2,8]{1,0:T(2,128)S(1)}, f32[2,8]{1,0:T(2,128)}, u32[]{:S(2)}) copy-start(f32[2,8]{1,0:T(2,128)} %get-tuple-element.5) | copy-start | bytes 196

commit v3 on v2

--- a/solution.py
+++ b/solution.py
@@ -9,8 +9,11 @@
 
 ITERS = 10
 EARLY = 4
-PASSES = 6
+PASSES = 7
 PIECES = 4
+DIRECT = 3
+LATER = 8
+HOOKS = (((), (), (0,), (1,), (2, 3)), ((), (), (), (), (0, 1, 2, 3)))
 MESH = pl.DeviceIdType.MESH
 
 
@@ -327,9 +330,9 @@
 
 
 def origin_kernel(
-    sizes, branch_in, count_in, walker_ref, trial_ref, chol_ref, field_ref, bias_ref, exch_ref,
-    branch_ref, count_ref, source, fields, chosen, outgoing, prop, trial, trial_t, chol, stack, green, lanes, sums, arrived,
-    own_sem, f_send, f_recv, t_send, t_recv, tx_send, tp_sem, cx_send, c_send, c_recv, cp_sem, w_send, w_recv, o_send, o_recv,
+    sizes, branch_in, walker_ref, trial_ref, chol_ref, field_ref, bias_ref, exch_ref,
+    branch_ref, source, fields, chosen, outgoing, prop, trial, trial_t, chol, stack, green, lanes, sums, arrived,
+    own_sem, f_send, f_recv, t_send, t_recv, tx_send, tp_sem, cx_send, cd_send, c_send, c_recv, cp_sem, w_send, w_recv, o_send, o_recv,
 ):
     walks, slabs, cores, slots, local, items = sizes
     walk, slab, core = lax.axis_index("walk"), lax.axis_index("slab"), lax.axis_index("row")
@@ -342,7 +345,7 @@
     below, above = walk > 0, walk < walks - 1
     steps = ((1, 1), (1, 0), (0, 1))
 
-    loads = [(branch_in, branch_ref), (count_in, count_ref), (walker_ref, source), (field_ref, fields.at[walk]), (trial_ref, trial.at[mine]), (chol_ref, chol.at[mine])]
+    loads = [(branch_in, branch_ref), (walker_ref, source), (field_ref, fields.at[walk]), (trial_ref, trial.at[mine]), (chol_ref, chol.at[mine])]
     own = [pltpu.make_async_copy(src, dst, own_sem.at[k]) for k, (src, dst) in enumerate(loads)]
     for copy in own:
         copy.start()
@@ -377,23 +380,27 @@
     def field_copy(o, way):
         return remote(fields.at[o], fields.at[o], f_send.at[way, o], f_recv.at[o], {"walk": walk + 1 - 2 * way})
 
-    def trial_view(q, o):
-        size = rows // walks
-        return trial.at[q, pl.ds(pl.multiple_of(o * size, size), size)]
+    half = lax.rem(walk, 2)
+
+    def trial_view(q, part):
+        size = rows // 2
+        return trial.at[q, pl.ds(pl.multiple_of(part * size, size), size)]
 
     def chol_rows(o, p):
         size = chol_ref.shape[0] // (walks * PIECES)
         return pl.ds(pl.multiple_of((o * PIECES + p) * size, size), size)
 
-    def trial_copy(o, way):
-        view = trial_view(across, o)
-        if way == 2:
-            return remote(view, view, t_send.at[2, o], t_recv.at[1, o], {"row": other_core})
-        return remote(view, view, t_send.at[way, o], t_recv.at[0, o], {"walk": walk + 1 - 2 * way})
-
-    def trial_beside(o):
-        view = trial_view(diagonal_q, o)
-        return remote(view, view, t_send.at[2, o], t_recv.at[1, o], {"row": other_core})
+    def trial_next(part):
+        view = trial_view(across, part)
+        return remote(view, view, t_send.at[0], t_recv.at[0, part], {"walk": walk + 1 - 2 * half})
+
+    def trial_relay(part):
+        view = trial_view(across, part)
+        return remote(view, view, t_send.at[1 + part], t_recv.at[1, part], {"row": other_core})
+
+    def trial_beside(part):
+        view = trial_view(diagonal_q, part)
+        return remote(view, view, t_send.at[1 + part], t_recv.at[1, part], {"row": other_core})
 
     def chol_copy(o, p, way):
         view = chol.at[across, chol_rows(o, p)]
@@ -406,7 +413,8 @@
         return remote(view, view, c_send.at[2, o, p], c_recv.at[1, o, p], {"row": other_core})
 
     def trial_across():
-        return remote(trial_view(mine, walk), trial_view(mine, walk), tx_send.at[0], t_recv.at[0, walk], {"slab": other_slab})
+        view = trial_view(mine, half)
+        return remote(view, view, tx_send.at[0], t_recv.at[0, half], {"slab": other_slab})
 
     def chol_across(p):
         return remote(chol.at[mine, chol_rows(walk, p)], chol.at[mine, chol_rows(walk, p)], cx_send.at[p], c_recv.at[0, walk, p], {"slab": other_slab})
@@ -438,20 +446,24 @@
 
     def field_hop(k):
         hop(k, lambda o: field_copy(o, 0).wait_recv(), lambda o, way: field_copy(o, way).start())
-
-    def trial_arrive(o):
-        trial_copy(o, 0).wait_recv()
-        trial_copy(o, 2).start()
-
-    def trial_hop(k):
-        hop(k, trial_arrive, lambda o, way: trial_copy(o, way).start())
 
     def chol_hop(k, p):
         def arrive(o):
             chol_copy(o, p, 0).wait_recv()
             chol_copy(o, p, 2).start()
 
-        hop(k, arrive, lambda o, way: chol_copy(o, p, way).start())
+        def forward(o, way):
+            if k < walks - 2 or p < PIECES - DIRECT:
+                chol_copy(o, p, way).start()
+
+        hop(k, arrive, forward)
+
+    def chol_direct(p, action):
+        if walks > 2:
+            far = walks - 1 - walk
+            view = chol.at[mine, chol_rows(far, p)]
+            copy = remote(view, view, cd_send.at[p], c_recv.at[0, far, p], {"slab": other_slab})
+            pl.when(jnp.logical_not(above & below))(lambda: action(copy))
 
     def chol_start(p):
         chol_copy(walk, p, 0).wait_recv()
@@ -506,41 +518,41 @@
                     prop[r, my_rows] = outgoing[r, row]
 
     both_ways(lambda way: field_copy(walk, way).start())
+    chol_across(0).start()
     trial_across().start()
-    for p in range(PIECES):
+    for p in range(1, PIECES):
         chol_across(p).start()
     trial_whole.start()
     chol_whole.start()
 
     last = walks - 1
     field_hop(1)
-    trial_arrive(walk)
-    both_ways(lambda way: trial_copy(walk, way).start())
     chol_start(0)
     for k in range(2, last):
         field_hop(k)
+    trial_next(half).wait_recv()
+    trial_next(half).start()
+    trial_relay(half).start()
     send_group(0, 1)
-    trial_hop(1)
     chol_start(1)
-    chol_start(2)
     if last > 1:
         field_hop(last)
     send_group(0, 0)
-    if last > 1:
-        trial_hop(2)
     send_group(1, 0)
     send_group(1, 1)
+    for p in range(PIECES - DIRECT, PIECES):
+        chol_direct(p, lambda copy: copy.start())
+    if last > 2:
+        chol_hop(1, 0)
+    chol_start(2)
+    trial_next(1 - half).wait_recv()
+    trial_relay(1 - half).start()
     chol_start(3)
     for k in range(1, last - 1):
-        for p in range(PIECES):
+        for p in range(1 if k == 1 else 0, PIECES):
             chol_hop(k, p)
-    for k in range(3, walks):
-        trial_hop(k)
-
-    @pl.loop(0, walks)
-    def _(o):
-        trial_beside(o).wait_recv()
-
+    for part in range(2):
+        trial_beside(part).wait_recv()
     trial_whole.wait_recv()
     for q in range(shards):
         trial_t[:, q * rows : (q + 1) * rows] = jnp.transpose(trial[q].astype(jnp.float32)).astype(jnp.bfloat16)
@@ -571,12 +583,15 @@
 
         hooks[2]()
 
-        @pl.loop(PASSES, ITERS)
-        def _(iteration):
-            both = stack[...]
-            stack[...] = 2.0 * both - dot3(both, both[electrons:, :])
-
-        hooks[3]()
+        for first, end, hook in ((PASSES, LATER, 3), (LATER, ITERS, 4)):
+
+            @pl.loop(first, end)
+            def _(iteration):
+                both = stack[...]
+                stack[...] = 2.0 * both - dot3(both, both[electrons:, :])
+
+            hooks[hook]()
+
         green[r] = dot(prop[r], stack[0:electrons, :].astype(jnp.bfloat16)).astype(jnp.bfloat16)
 
     blocks = (mine, beside, across, diagonal_q)
@@ -607,15 +622,25 @@
         def _():
             arrived[r * shards + mine] = sums[r]
 
-    def hooks_of(k):
-        return [functools.partial(chol_hop, k, p) for p in range(PIECES)] if k > 0 else [lambda: None] * PIECES
-
-    invert(0, hooks_of(last - 1))
+    def hooks_of(k, pieces):
+        def relay(group):
+            def run():
+                if k > 0:
+                    for p in group:
+                        chol_hop(k, p)
+
+            return run
+
+        return [relay(group) for group in pieces]
+
+    invert(0, hooks_of(last - 1 if last > 2 else 0, HOOKS[0]))
     contract(0, 0)
     chol_whole.wait_recv()
     contract(0, 1)
     for r in range(1, items):
-        invert(r, hooks_of(last) if r == 1 else hooks_of(0))
+        invert(r, hooks_of(last, HOOKS[1]) if r == 1 else hooks_of(0, HOOKS[1]))
+        contract(r, 0)
+        contract(r, 1)
     contract(0, 2)
 
     @pl.loop(0, walks)
@@ -627,7 +652,7 @@
     contract(0, 3)
     publish(0)
     for r in range(1, items):
-        for n in range(shards):
+        for n in range(2, shards):
             contract(r, n)
         publish(r)
 
@@ -660,21 +685,23 @@
             dx, dc = lax.rem(lax.div(q, cores) + slab, slabs), lax.rem(lax.rem(q, cores) + core, cores)
             first = (dx * cores + dc) * vectors
             total = jnp.where(column == j, arrived[numbers[j], kind, pl.ds(first, vectors), 0:slots], total)
-        result[...] = jnp.where(column < count_ref[0], total * (1.0, -0.5)[kind], 0.0)
+        result[...] = total
 
     trial_across().wait_send()
+    trial_next(half).wait_send()
+    for part in range(2):
+        trial_relay(part).wait_send()
     trial_whole.wait_send()
+    for p in range(PIECES - DIRECT, PIECES):
+        chol_direct(p, lambda copy: copy.wait_send())
     chol_whole.wait_send()
     for p in range(PIECES):
         chol_across(p).wait_send()
 
     @pl.loop(0, walks)
     def _(o):
-        trial_copy(o, 2).wait_send()
-
         def sent(way):
             field_copy(o, way).wait_send()
-            trial_copy(o, way).wait_send()
 
         pl.when(above & (o <= walk))(lambda: sent(0))
         pl.when(below & (o >= walk))(lambda: sent(1))
@@ -682,8 +709,10 @@
         @pl.loop(0, PIECES)
         def _(p):
             chol_copy(o, p, 2).wait_send()
-            pl.when(above & (o <= walk))(lambda: chol_copy(o, p, 0).wait_send())
-            pl.when(below & (o >= walk))(lambda: chol_copy(o, p, 1).wait_send())
+            chained = (p < PIECES - DIRECT) | (walks < 3)
+            upward, downward = (o > 0) | (walk < walks - 2), (o < walks - 1) | (walk > 1)
+            pl.when(above & (o <= walk) & (chained | upward))(lambda: chol_copy(o, p, 0).wait_send())
+            pl.when(below & (o >= walk) & (chained | downward))(lambda: chol_copy(o, p, 1).wait_send())
 
     for r in range(items):
         for dx, dc in steps:
@@ -763,7 +792,7 @@
     return bias, exchange
 
 
-def at_origin(walkers, trial_orbitals, cholesky, branches, counts, field):
+def at_origin(walkers, trial_orbitals, cholesky, branches, field):
     walks, slabs, cores = lax.axis_size("walk"), lax.axis_size("slab"), lax.axis_size("row")
     slots, rows, electrons = walkers.shape
     vectors = cholesky.shape[0]
@@ -774,11 +803,10 @@
     bias, exchange = pl.pallas_call(
         functools.partial(origin_kernel, (walks, slabs, cores, slots, local, items)),
         out_shape=[jax.ShapeDtypeStruct((vectors, slots), jnp.float32)] * 2,
-        in_specs=[pl.BlockSpec(memory_space=pl.ANY)] * 6,
+        in_specs=[pl.BlockSpec(memory_space=pltpu.HBM)] * 5,
         out_specs=[vmem] * 2,
         scratch_shapes=[
             pltpu.SMEM(branches.shape, jnp.int32),
-            pltpu.SMEM(counts.shape, jnp.int32),
             pltpu.VMEM((slots, rows, electrons), jnp.bfloat16),
             pltpu.VMEM((walks, slots, rows), jnp.float32),
             pltpu.VMEM((slots, rows), jnp.float32),
@@ -792,17 +820,17 @@
             pltpu.VMEM((items, 2, shards * vectors, electrons), jnp.float32),
             pltpu.VMEM((items, 2, shards * vectors, 128), jnp.float32),
             pltpu.VMEM((slots, 2, shards * vectors, 128), jnp.float32),
-            dma((6,)),
+            dma((5,)),
             dma((2, walks)), dma((walks,)),
-            dma((3, walks)), dma((2, walks)), dma((2,)), dma((2,)),
-            dma((PIECES,)), dma((3, walks, PIECES)), dma((2, walks, PIECES)), dma((2,)),
+            dma((3,)), dma((2, 2)), dma((2,)), dma((2,)),
+            dma((PIECES,)), dma((PIECES,)), dma((3, walks, PIECES)), dma((2, walks, PIECES)), dma((2,)),
             dma((items, shards)), dma((items, shards)),
             dma((items, shards)), dma((slots,)),
         ],
         compiler_params=pltpu.CompilerParams(
-            collective_id=0, has_side_effects=True, vmem_limit_bytes=60 * 1024 * 1024
+            collective_id=0, has_side_effects=True, vmem_limit_bytes=55200 * 1024
         ),
-    )(branches, counts, walkers, trial_orbitals, cholesky.reshape(lines, columns), field)
+    )(branches, walkers, trial_orbitals, cholesky.reshape(lines, columns), field)
     return bias.T, exchange.T
 
 
@@ -811,10 +839,11 @@
     slots, rows, electrons = walkers.shape
     lines = cholesky.shape[0] * electrons
     even = walks & (walks - 1) == 0 and slots % walks == 0 and slots % (slabs * cores) == 0
-    whole = lines % (walks * PIECES * 16) == 0 and rows % (walks * 16) == 0
+    whole = lines % (walks * PIECES * 16) == 0 and rows % 32 == 0 and walks > 2
     if slabs == cores == 2 and slots == 2 * walks and PIECES == 4 and even and whole:
-        return at_origin(walkers, trial_orbitals, cholesky, branches, counts, field)
-    bias, exchange = gathered(walkers, trial_orbitals, cholesky, branches, field)
+        bias, exchange = at_origin(walkers, trial_orbitals, cholesky, branches, field)
+    else:
+        bias, exchange = gathered(walkers, trial_orbitals, cholesky, branches, field)
     living = (jnp.arange(slots, dtype=jnp.int32) < counts[0]).astype(jnp.float32)[:, None]
     return bias * living, -0.5 * exchange * living
 

time: 41.6 us -> 39.9 us (0.959)
  local copies, waits for them, and re-layouts: 1.85 us -> 0.63 us
  Pallas kernels: 38.2 us -> 37.1 us
  other arithmetic: 0 us -> 0.58 us
    unnamed x6 -> x4, local copies, waits for them, and re-layouts: 1.85 us -> 0.63 us
    pallas_call x1, Pallas kernels: 38.2 us -> 37.1 us  [at_origin(): pl.pallas_call(functools.partial(origin_kernel, (walks, slabs, cores, slo...]
    mul x0 -> x2, other arithmetic: none -> 0.57 us  [on_device(): return (bias * living, -0.5 * exchange * living)]
where the time goes in v3:
time: 39.9 us; the launch traced here: 39.7 us
  Pallas kernels  37.1 us (93%)
  between operations  1.34 us (3%)
  local copies, waits for them, and re-layouts  0.63 us (2%)
  other arithmetic  0.58 us (1%)
    pallas_call x1, Pallas kernels, at_origin(): pl.pallas_call(functools.partial(origin_kernel, (walks, slabs, cores, slo...  37.1 us

profile of v3, /device:TPU:0, one launch (start us, length us, event | category | flops | bytes accessed | tf_op | source)
XLA Modules:
  0.0 39.7 jit_solution(12964018378988959843)
XLA Ops:
  0.6 0.0 copy-start
  1.3 0.0 copy-start.1
  1.3 0.0 copy-done
  1.3 0.6 %copy-done.1 = s32[32]{0:T(128)S(1)} copy-done((s32[32]{0:T(128)S(1)}, s32[32]{0:T(128)}, u32[]{:S(2)}) %copy-start.1) | copy-done | bytes 152
  2.0 37.1 %shard_map.77 = (f32[2,8]{1,0:T(2,128)S(1)}, f32[2,8]{1,0:T(2,128)S(1)}) custom-call(s32[32]{0:T(128)S(1)} %copy-done.1, bf16[8,256,256]{2,1,0:T(8,128)(2,1)} %walker_ref.1, bf16[256,256]{1,0:T(8,128)(2,1)} %trial_ref.1, bf16[512,1024]{1,0:T(8,128)(2,1)} %bitcast.8, f32[8,256]{1,0:T(8,128)S(1)} %copy-done), custom_call_target="tpu_custom_call" | custom-call | tf_op jit(solution)/shard_map/pallas_call | solution.py:803
  39.1 0.6 %multiply_bitcast_fusion = (f32[8,2]{0,1:T(2,128)}, f32[8,2]{0,1:T(2,128)}) fusion(f32[2,8]{1,0:T(2,128)S(1)} %get-tuple-element.5, f32[8]{0:T(128)S(1)} %compare_select_fusion, f32[2,8]{1,0:T(2,128)S(1)} %get-tuple-element.4, f32[8]{0:T(128)S(1)} %compare_convert_fusion), kind=kLoop, calls=%fused_computation.2 | loop fusion | flops 32 | bytes 320 | tf_op jit(solution)/shard_map/mul | solution.py:848
  (2 shorter events, 0.0 us)
Async XLA Ops:
  0.6 0.7 %copy-start = (f32[8,256]{1,0:T(8,128)S(1)}, f32[8,256]{1,0:T(8,128)}, u32[]{:S(2)}) copy-start(f32[8,256]{1,0:T(8,128)} %field_ref.1) | copy-start | bytes 24580
  1.3 0.7 %copy-start.1 = (s32[32]{0:T(128)S(1)}, s32[32]{0:T(128)}, u32[]{:S(2)}) copy-start(s32[32]{0:T(128)} %branch_in.1) | copy-start | bytes 388

commit v4 on v3

--- a/solution.py
+++ b/solution.py
@@ -330,7 +330,7 @@
 
 
 def origin_kernel(
-    sizes, branch_in, walker_ref, trial_ref, chol_ref, field_ref, bias_ref, exch_ref,
+    sizes, branch_in, walker_ref, trial_ref, chol_ref, field_ref, bias_ref, exch_ref, living_ref,
     branch_ref, source, fields, chosen, outgoing, prop, trial, trial_t, chol, stack, green, lanes, sums, arrived,
     own_sem, f_send, f_recv, t_send, t_recv, tx_send, tp_sem, cx_send, cd_send, c_send, c_recv, cp_sem, w_send, w_recv, o_send, o_recv,
 ):
@@ -639,8 +639,6 @@
     contract(0, 1)
     for r in range(1, items):
         invert(r, hooks_of(last, HOOKS[1]) if r == 1 else hooks_of(0, HOOKS[1]))
-        contract(r, 0)
-        contract(r, 1)
     contract(0, 2)
 
     @pl.loop(0, walks)
@@ -652,7 +650,7 @@
     contract(0, 3)
     publish(0)
     for r in range(1, items):
-        for n in range(2, shards):
+        for n in range(shards):
             contract(r, n)
         publish(r)
 
@@ -686,6 +684,7 @@
             first = (dx * cores + dc) * vectors
             total = jnp.where(column == j, arrived[numbers[j], kind, pl.ds(first, vectors), 0:slots], total)
         result[...] = total
+    living_ref[...] = jnp.where(column < branch_ref[walks * slots], 1.0, 0.0)
 
     trial_across().wait_send()
     trial_next(half).wait_send()
@@ -792,7 +791,7 @@
     return bias, exchange
 
 
-def at_origin(walkers, trial_orbitals, cholesky, branches, field):
+def at_origin(walkers, trial_orbitals, cholesky, branches, counts, field):
     walks, slabs, cores = lax.axis_size("walk"), lax.axis_size("slab"), lax.axis_size("row")
     slots, rows, electrons = walkers.shape
     vectors = cholesky.shape[0]
@@ -800,13 +799,14 @@
     items, lines, columns = slots // shards, vectors * electrons, shards * rows
     dma = pltpu.SemaphoreType.DMA
     vmem = pl.BlockSpec(memory_space=pltpu.VMEM)
-    bias, exchange = pl.pallas_call(
+    numbers = jnp.concatenate([branches, counts])
+    bias, exchange, living = pl.pallas_call(
         functools.partial(origin_kernel, (walks, slabs, cores, slots, local, items)),
-        out_shape=[jax.ShapeDtypeStruct((vectors, slots), jnp.float32)] * 2,
+        out_shape=[jax.ShapeDtypeStruct((vectors, slots), jnp.float32)] * 3,
         in_specs=[pl.BlockSpec(memory_space=pltpu.HBM)] * 5,
-        out_specs=[vmem] * 2,
+        out_specs=[vmem] * 3,
         scratch_shapes=[
-            pltpu.SMEM(branches.shape, jnp.int32),
+            pltpu.SMEM(numbers.shape, jnp.int32),
             pltpu.VMEM((slots, rows, electrons), jnp.bfloat16),
             pltpu.VMEM((walks, slots, rows), jnp.float32),
             pltpu.VMEM((slots, rows), jnp.float32),
@@ -828,10 +828,10 @@
             dma((items, shards)), dma((slots,)),
         ],
         compiler_params=pltpu.CompilerParams(
-            collective_id=0, has_side_effects=True, vmem_limit_bytes=55200 * 1024
+            collective_id=0, has_side_effects=True, vmem_limit_bytes=55216 * 1024
         ),
-    )(branches, walkers, trial_orbitals, cholesky.reshape(lines, columns), field)
-    return bias.T, exchange.T
+    )(numbers, walkers, trial_orbitals, cholesky.reshape(lines, columns), field)
+    return (bias * living).T, (-0.5 * exchange * living).T
 
 
 def on_device(walkers, trial_orbitals, cholesky, branches, counts, field):
@@ -841,9 +841,8 @@
     even = walks & (walks - 1) == 0 and slots % walks == 0 and slots % (slabs * cores) == 0
     whole = lines % (walks * PIECES * 16) == 0 and rows % 32 == 0 and walks > 2
     if slabs == cores == 2 and slots == 2 * walks and PIECES == 4 and even and whole:
-        bias, exchange = at_origin(walkers, trial_orbitals, cholesky, branches, field)
-    else:
-        bias, exchange = gathered(walkers, trial_orbitals, cholesky, branches, field)
+        return at_origin(walkers, trial_orbitals, cholesky, branches, counts, field)
+    bias, exchange = gathered(walkers, trial_orbitals, cholesky, branches, field)
     living = (jnp.arange(slots, dtype=jnp.int32) < counts[0]).astype(jnp.float32)[:, None]
     return bias * living, -0.5 * exchange * living
 

time: 39.9 us -> 39 us (0.977)
  local copies, waits for them, and re-layouts: 0.63 us -> 0.01 us
    unnamed x4 -> x2, local copies, waits for them, and re-layouts: 0.63 us -> 0.01 us
    mul x2 -> x0, other arithmetic: 0.57 us -> none  [on_device(): return (bias * living, -0.5 * exchange * living)]
    transpose x0 -> x1, other arithmetic: none -> 0.57 us  [at_origin(): return ((bias * living).T, (-0.5 * exchange * living).T)]
where the time goes in v4:
time: 39 us; the launch traced here: 38.8 us
  Pallas kernels  36.9 us (95%)
  between operations  1.31 us (3%)
  other arithmetic  0.65 us (2%)
    pallas_call x1, Pallas kernels, at_origin(): pl.pallas_call(functools.partial(origin_kernel, (walks, slabs, cores, slo...  36.9 us

profile of v4, /device:TPU:0, one launch (start us, length us, event | category | flops | bytes accessed | tf_op | source)
XLA Modules:
  0.0 38.8 jit_solution(592765743139220918)
XLA Ops:
  0.6 0.0 copy-start
  1.3 0.0 copy-done
  1.3 0.1 pad_add_fusion.branch_in
  1.4 36.9 %shard_map.77 = (f32[2,8]{1,0:T(2,128)S(1)}, f32[2,8]{1,0:T(2,128)S(1)}, f32[2,8]{1,0:T(2,128)S(1)}) custom-call(s32[33]{0:T(128)S(1)} %pad_add_fusion.branch_in, bf16[8,256,256]{2,1,0:T(8,128)(2,1)} %walker_ref.1, bf16[256,256]{1,0:T(8,128)(2,1)} %trial_ref.1, bf16[512,1024]{1,0:T(8,128)(2,1)} %bitcast.5, f32[8,256]{1,0:T(8,128)} %field_ref.1), custom_call_target="tpu_custom_call" | custom-call | tf_op jit(solution)/shard_map/pallas_call | solution.py:803
  38.2 0.6 %multiply_bitcast_fusion = (f32[8,2]{0,1:T(2,128)}, f32[8,2]{0,1:T(2,128)}) fusion(f32[2,8]{1,0:T(2,128)S(1)} %get-tuple-element.6, f32[2,8]{1,0:T(2,128)S(1)} %get-tuple-element.7, f32[2,8]{1,0:T(2,128)S(1)} %get-tuple-element.5), kind=kLoop, calls=%fused_computation | loop fusion | flops 48 | bytes 320 | tf_op jit(solution)/shard_map/transpose | solution.py:834
Async XLA Ops:
  0.6 0.7 %copy-start = (s32[32]{0:T(128)S(1)}, s32[32]{0:T(128)}, u32[]{:S(2)}) copy-start(s32[32]{0:T(128)} %param.9) | copy-start | bytes 388

commit v5 on v4

--- a/solution.py
+++ b/solution.py
@@ -640,6 +640,8 @@
     for r in range(1, items):
         invert(r, hooks_of(last, HOOKS[1]) if r == 1 else hooks_of(0, HOOKS[1]))
     contract(0, 2)
+    for r in range(1, items):
+        contract(r, 0)
 
     @pl.loop(0, walks)
     def _(o):
@@ -650,7 +652,7 @@
     contract(0, 3)
     publish(0)
     for r in range(1, items):
-        for n in range(shards):
+        for n in range(1, shards):
             contract(r, n)
         publish(r)
 

time: 39 us -> 39 us (level)
  no operation moved by 1% of the time
where the time goes in v5:
time: 39 us; the launch traced here: 38.8 us
  Pallas kernels  36.8 us (94%)
  between operations  1.31 us (3%)
  other arithmetic  0.65 us (2%)
    pallas_call x1, Pallas kernels, at_origin(): pl.pallas_call(functools.partial(origin_kernel, (walks, slabs, cores, slo...  36.8 us

profile of v5, /device:TPU:0, one launch (start us, length us, event | category | flops | bytes accessed | tf_op | source)
XLA Modules:
  0.0 38.8 jit_solution(562325227187546795)
XLA Ops:
  0.6 0.0 copy-start
  1.3 0.0 copy-done
  1.3 0.1 pad_add_fusion.branch_in
  1.4 36.8 %shard_map.77 = (f32[2,8]{1,0:T(2,128)S(1)}, f32[2,8]{1,0:T(2,128)S(1)}, f32[2,8]{1,0:T(2,128)S(1)}) custom-call(s32[33]{0:T(128)S(1)} %pad_add_fusion.branch_in, bf16[8,256,256]{2,1,0:T(8,128)(2,1)} %walker_ref.1, bf16[256,256]{1,0:T(8,128)(2,1)} %trial_ref.1, bf16[512,1024]{1,0:T(8,128)(2,1)} %bitcast.5, f32[8,256]{1,0:T(8,128)} %field_ref.1), custom_call_target="tpu_custom_call" | custom-call | tf_op jit(solution)/shard_map/pallas_call | solution.py:805
  38.2 0.6 %multiply_bitcast_fusion = (f32[8,2]{0,1:T(2,128)}, f32[8,2]{0,1:T(2,128)}) fusion(f32[2,8]{1,0:T(2,128)S(1)} %get-tuple-element.6, f32[2,8]{1,0:T(2,128)S(1)} %get-tuple-element.7, f32[2,8]{1,0:T(2,128)S(1)} %get-tuple-element.5), kind=kLoop, calls=%fused_computation | loop fusion | flops 48 | bytes 320 | tf_op jit(solution)/shard_map/transpose | solution.py:836
Async XLA Ops:
  0.6 0.7 %copy-start = (s32[32]{0:T(128)S(1)}, s32[32]{0:T(128)}, u32[]{:S(2)}) copy-start(s32[32]{0:T(128)} %param.9) | copy-start | bytes 388

commit v6 on v4

--- a/solution.py
+++ b/solution.py
@@ -347,8 +347,6 @@
 
     loads = [(branch_in, branch_ref), (walker_ref, source), (field_ref, fields.at[walk]), (trial_ref, trial.at[mine]), (chol_ref, chol.at[mine])]
     own = [pltpu.make_async_copy(src, dst, own_sem.at[k]) for k, (src, dst) in enumerate(loads)]
-    for copy in own:
-        copy.start()
     barrier = pltpu.get_barrier_semaphore()
 
     def greet(target):
@@ -368,6 +366,8 @@
     def _():
         greet({"walk": walk + 1})
 
+    for copy in own:
+        copy.start()
     for copy in own:
         copy.wait()
     pl.semaphore_wait(barrier, len(steps) + jnp.where(below, 1, 0) + jnp.where(above, 1, 0))

time: 39 us -> 39 us (level)
  no operation moved by 1% of the time
where the time goes in v6:
time: 39 us; the launch traced here: 38.9 us
  Pallas kernels  36.9 us (95%)
  between operations  1.31 us (3%)
  other arithmetic  0.65 us (2%)
    pallas_call x1, Pallas kernels, at_origin(): pl.pallas_call(functools.partial(origin_kernel, (walks, slabs, cores, slo...  36.9 us

profile of v6, /device:TPU:0, one launch (start us, length us, event | category | flops | bytes accessed | tf_op | source)
XLA Modules:
  0.0 38.9 jit_solution(8006403386072994597)
XLA Ops:
  0.6 0.0 copy-start
  1.3 0.0 copy-done
  1.3 0.1 pad_add_fusion.branch_in
  1.4 36.9 %shard_map.77 = (f32[2,8]{1,0:T(2,128)S(1)}, f32[2,8]{1,0:T(2,128)S(1)}, f32[2,8]{1,0:T(2,128)S(1)}) custom-call(s32[33]{0:T(128)S(1)} %pad_add_fusion.branch_in, bf16[8,256,256]{2,1,0:T(8,128)(2,1)} %walker_ref.1, bf16[256,256]{1,0:T(8,128)(2,1)} %trial_ref.1, bf16[512,1024]{1,0:T(8,128)(2,1)} %bitcast.5, f32[8,256]{1,0:T(8,128)} %field_ref.1), custom_call_target="tpu_custom_call" | custom-call | tf_op jit(solution)/shard_map/pallas_call | solution.py:803
  38.3 0.6 %multiply_bitcast_fusion = (f32[8,2]{0,1:T(2,128)}, f32[8,2]{0,1:T(2,128)}) fusion(f32[2,8]{1,0:T(2,128)S(1)} %get-tuple-element.6, f32[2,8]{1,0:T(2,128)S(1)} %get-tuple-element.7, f32[2,8]{1,0:T(2,128)S(1)} %get-tuple-element.5), kind=kLoop, calls=%fused_computation | loop fusion | flops 48 | bytes 320 | tf_op jit(solution)/shard_map/transpose | solution.py:834
Async XLA Ops:
  0.6 0.7 %copy-start = (s32[32]{0:T(128)S(1)}, s32[32]{0:T(128)}, u32[]{:S(2)}) copy-start(s32[32]{0:T(128)} %param.9) | copy-start | bytes 388

commit v7 on v4

--- a/solution.py
+++ b/solution.py
@@ -535,6 +535,8 @@
     trial_relay(half).start()
     send_group(0, 1)
     chol_start(1)
+    if last > 2:
+        chol_hop(1, 0)
     if last > 1:
         field_hop(last)
     send_group(0, 0)
@@ -542,8 +544,6 @@
     send_group(1, 1)
     for p in range(PIECES - DIRECT, PIECES):
         chol_direct(p, lambda copy: copy.start())
-    if last > 2:
-        chol_hop(1, 0)
     chol_start(2)
     trial_next(1 - half).wait_recv()
     trial_relay(1 - half).start()

time: 39 us -> 38.9 us (level)
  no operation moved by 1% of the time
where the time goes in v7:
time: 38.9 us; the launch traced here: 38.8 us
  Pallas kernels  36.8 us (95%)
  between operations  1.31 us (3%)
  other arithmetic  0.65 us (2%)
    pallas_call x1, Pallas kernels, at_origin(): pl.pallas_call(functools.partial(origin_kernel, (walks, slabs, cores, slo...  36.8 us

profile of v7, /device:TPU:0, one launch (start us, length us, event | category | flops | bytes accessed | tf_op | source)
XLA Modules:
  0.0 38.8 jit_solution(15422868191846009432)
XLA Ops:
  0.6 0.0 copy-start
  1.3 0.0 copy-done
  1.3 0.1 pad_add_fusion.branch_in
  1.4 36.8 %shard_map.77 = (f32[2,8]{1,0:T(2,128)S(1)}, f32[2,8]{1,0:T(2,128)S(1)}, f32[2,8]{1,0:T(2,128)S(1)}) custom-call(s32[33]{0:T(128)S(1)} %pad_add_fusion.branch_in, bf16[8,256,256]{2,1,0:T(8,128)(2,1)} %walker_ref.1, bf16[256,256]{1,0:T(8,128)(2,1)} %trial_ref.1, bf16[512,1024]{1,0:T(8,128)(2,1)} %bitcast.5, f32[8,256]{1,0:T(8,128)} %field_ref.1), custom_call_target="tpu_custom_call" | custom-call | tf_op jit(solution)/shard_map/pallas_call | solution.py:803
  38.2 0.6 %multiply_bitcast_fusion = (f32[8,2]{0,1:T(2,128)}, f32[8,2]{0,1:T(2,128)}) fusion(f32[2,8]{1,0:T(2,128)S(1)} %get-tuple-element.6, f32[2,8]{1,0:T(2,128)S(1)} %get-tuple-element.7, f32[2,8]{1,0:T(2,128)S(1)} %get-tuple-element.5), kind=kLoop, calls=%fused_computation | loop fusion | flops 48 | bytes 320 | tf_op jit(solution)/shard_map/transpose | solution.py:834
Async XLA Ops:
  0.6 0.7 %copy-start = (s32[32]{0:T(128)S(1)}, s32[32]{0:T(128)}, u32[]{:S(2)}) copy-start(s32[32]{0:T(128)} %param.9) | copy-start | bytes 388
